TPU v7x, 32 devices: a whole 2x2x4 slice. The times are simulated.
32 devices in a mesh: dp: 2 (over x), ts: 16 (over z, y, core).
Axes of the slice: x: 2, y: 2, z: 4, core: 2. Of those that a mesh axis runs over, the one named last changes fastest.
Arguments:
- clip_video: bfloat16 [64, 4, 40, 128], P(('dp', 'ts')), may hold values from -6 to 6
- conv_weight: bfloat16 [3, 3, 3, 128, 128], replicated, may hold values from -0.109375 to 0.109375
- embed_weight: bfloat16 [128, 5120], replicated, may hold values from -0.5 to 0.5
- gain_spatial: float32 [5120], replicated, may hold values from 0.5 to 1.5
- gain_temporal: float32 [5120], replicated, may hold values from 0.5 to 1.5
- input_spatial: bfloat16 [5120, 384], P(('dp', 'ts')), may hold values from -0.078125 to 0.078125
- input_temporal: bfloat16 [5120, 384], P(('dp', 'ts')), may hold values from -0.078125 to 0.078125
- output_spatial: bfloat16 [128, 5120], replicated, may hold values from -2 to 2
- output_temporal: bfloat16 [128, 5120], replicated, may hold values from -2 to 2
- cotangent: bfloat16 [64, 4, 40, 5120], P(('dp', 'ts')), may hold values from -6 to 6
Outputs:
- layer_output: bfloat16 [64, 4, 40, 5120], P(('dp', 'ts'))
- grad_spatial: float32 [5120, 384], P(('dp', 'ts'))
All inputs are finite; a program needn't handle non-finite values.
Results may differ from a plain program's by a relative error of at most 0.015.
Values may be sent and summed in bfloat16 or wider, within the bound.
A program may use at most 128 MiB of HBM per device.

v0:
```python
import jax
import jax.numpy as jnp
from jax import lax
from jax.sharding import PartitionSpec as P

FR = 16


epsilon = 1e-06
masked = -1e30


def passed_along(block, axis, distance):
    devices = range(lax.axis_size(axis))
    route = [(i - distance, i) for i in devices if i - distance in devices]
    return lax.ppermute(block, axis, route)


def conv_local(volume, weight, count):
    frames, height, columns, channels = volume.shape
    out_channels = weight.shape[-1]
    padded = jnp.pad(volume, ((0, 0), (1, 1), (1, 1), (0, 0)))
    summed = jnp.zeros((count * height * columns, out_channels), jnp.float32)
    for time_tap in range(3):
        for row_tap in range(3):
            for col_tap in range(3):
                window = padded[
                    2 - time_tap : 2 - time_tap + count,
                    row_tap : row_tap + height,
                    col_tap : col_tap + columns,
                    :,
                ]
                summed = summed + jnp.dot(
                    window.reshape(-1, channels),
                    weight[time_tap, row_tap, col_tap],
                    preferred_element_type=jnp.float32,
                )
    return summed.reshape(count, height, columns, out_channels)


def rms_norm(hidden, norm_gain):
    widened = hidden.astype(jnp.float32)
    factor = lax.rsqrt(jnp.mean(widened * widened, axis=-1, keepdims=True) + epsilon)
    return ((widened * factor * norm_gain).astype(jnp.bfloat16), factor)


def rms_norm_grad(hidden, norm_gain, factor, upstream):
    widened = hidden.astype(jnp.float32)
    scaled = upstream * norm_gain
    inner_mean = jnp.mean(widened * scaled, axis=-1, keepdims=True)
    return factor * scaled - widened * factor**3 * inner_mean


def frame_forward(packed):
    frames, places, triple = packed.shape
    head_size = triple // 3
    queries = packed[..., :head_size]
    key_rows = packed[..., head_size : 2 * head_size]
    values = packed[..., 2 * head_size :]
    scores = jnp.einsum(
        "fqd,fkd->fqk", queries, key_rows, preferred_element_type=jnp.float32
    ) * head_size ** (-0.5)
    attend = jax.nn.softmax(scores, axis=-1)
    rounded = attend.astype(jnp.bfloat16)
    mixture = jnp.einsum("fqk,fkd->fqd", rounded, values, preferred_element_type=jnp.float32)
    return (mixture.astype(jnp.bfloat16), attend)


def frame_backward(packed, attend, upstream):
    frames, places, triple = packed.shape
    head_size = triple // 3
    scale_factor = head_size ** (-0.5)
    queries = packed[..., :head_size]
    key_rows = packed[..., head_size : 2 * head_size]
    values = packed[..., 2 * head_size :]
    rounded = attend.astype(jnp.bfloat16)
    grad_attend = jnp.einsum("fqd,fkd->fqk", upstream, values, preferred_element_type=jnp.float32)
    grad_values = jnp.einsum("fqk,fqd->fkd", rounded, upstream, preferred_element_type=jnp.float32)
    grad_scores = attend * (grad_attend - jnp.sum(grad_attend * attend, axis=-1, keepdims=True))
    grad_rounded = grad_scores.astype(jnp.bfloat16)
    grad_queries = (
        jnp.einsum("fqk,fkd->fqd", grad_rounded, key_rows, preferred_element_type=jnp.float32)
        * scale_factor
    )
    grad_keys = (
        jnp.einsum("fqk,fqd->fkd", grad_rounded, queries, preferred_element_type=jnp.float32)
        * scale_factor
    )
    joined = jnp.concatenate([grad_queries, grad_keys, grad_values], axis=-1)
    return joined.astype(jnp.bfloat16)


def clip_forward(packed):
    frames, places, triple = packed.shape
    head_size = triple // 3
    volume = packed.reshape(frames // FR, FR, places, triple)
    queries = volume[..., :head_size]
    key_rows = volume[..., head_size : 2 * head_size]
    values = volume[..., 2 * head_size :]
    scores = jnp.einsum(
        "cqpd,ckpd->cpqk", queries, key_rows, preferred_element_type=jnp.float32
    ) * head_size ** (-0.5)
    allowed = jnp.arange(FR)[:, None] >= jnp.arange(FR)[None, :]
    scores = jnp.where(allowed, scores, masked)
    attend = jax.nn.softmax(scores, axis=-1)
    rounded = attend.astype(jnp.bfloat16)
    mixture = jnp.einsum("cpqk,ckpd->cqpd", rounded, values, preferred_element_type=jnp.float32)
    return (mixture.astype(jnp.bfloat16).reshape(frames, places, head_size), attend)


def clip_backward(packed, attend, upstream):
    frames, places, triple = packed.shape
    head_size = triple // 3
    scale_factor = head_size ** (-0.5)
    volume = packed.reshape(frames // FR, FR, places, triple)
    queries = volume[..., :head_size]
    key_rows = volume[..., head_size : 2 * head_size]
    values = volume[..., 2 * head_size :]
    grad_out = upstream.reshape(frames // FR, FR, places, head_size)
    rounded = attend.astype(jnp.bfloat16)
    grad_attend = jnp.einsum(
        "cqpd,ckpd->cpqk", grad_out, values, preferred_element_type=jnp.float32
    )
    grad_values = jnp.einsum(
        "cpqk,cqpd->ckpd", rounded, grad_out, preferred_element_type=jnp.float32
    )
    grad_scores = attend * (grad_attend - jnp.sum(grad_attend * attend, axis=-1, keepdims=True))
    grad_rounded = grad_scores.astype(jnp.bfloat16)
    grad_queries = (
        jnp.einsum("cpqk,ckpd->cqpd", grad_rounded, key_rows, preferred_element_type=jnp.float32)
        * scale_factor
    )
    grad_keys = (
        jnp.einsum("cpqk,cqpd->ckpd", grad_rounded, queries, preferred_element_type=jnp.float32)
        * scale_factor
    )
    joined = jnp.concatenate([grad_queries, grad_keys, grad_values], axis=-1)
    return joined.astype(jnp.bfloat16).reshape(frames, places, triple)


def shards(
    clip_video,
    conv_weight,
    embed_weight,
    gain_spatial,
    gain_temporal,
    input_spatial,
    input_temporal,
    output_spatial,
    output_temporal,
    cotangent,
):
    frames_here = clip_video.shape[0]
    prior = passed_along(clip_video, "ts", 1)
    opening = lax.axis_index("ts") == 0
    prior = jnp.where(opening, jnp.zeros_like(prior), prior)
    volume = jnp.concatenate([prior, clip_video], axis=0)
    whole_spatial, whole_temporal = (
        lax.all_gather(input_spatial, ("dp", "ts"), axis=0, tiled=True),
        lax.all_gather(input_temporal, ("dp", "ts"), axis=0, tiled=True),
    )
    features = jax.nn.gelu(conv_local(volume, conv_weight, frames_here), approximate=True).astype(
        jnp.bfloat16
    )
    frames, height, columns, channels = features.shape
    places = height * columns
    tokens = frames * places
    embedded = jnp.dot(
        features.reshape(tokens, channels), embed_weight, preferred_element_type=jnp.float32
    ).astype(jnp.bfloat16)
    normed_one, factor_one = rms_norm(embedded, gain_spatial)
    packed_one = jnp.dot(normed_one, whole_spatial, preferred_element_type=jnp.float32).astype(
        jnp.bfloat16
    )
    packed_one = packed_one.reshape(frames, places, -1)
    mixture_one, attend_one = frame_forward(packed_one)
    after_space = (
        embedded.astype(jnp.float32)
        + jnp.dot(
            mixture_one.reshape(tokens, -1), output_spatial, preferred_element_type=jnp.float32
        )
    ).astype(jnp.bfloat16)
    normed_two, factor_two = rms_norm(after_space, gain_temporal)
    packed_two = jnp.dot(normed_two, whole_temporal, preferred_element_type=jnp.float32).astype(
        jnp.bfloat16
    )
    packed_two = packed_two.reshape(frames, places, -1)
    cotangent_rows = cotangent.reshape(tokens, -1)
    grad_mix_two = jnp.dot(
        cotangent_rows, output_temporal.T, preferred_element_type=jnp.float32
    ).astype(jnp.bfloat16)
    grad_mix_two = grad_mix_two.reshape(frames, places, -1)
    patched = lax.all_to_all(packed_two, "ts", split_axis=1, concat_axis=0, tiled=True)
    mixture_patched, attend_two = clip_forward(patched)
    mixture_two = lax.all_to_all(mixture_patched, "ts", split_axis=0, concat_axis=1, tiled=True)
    grad_patched = lax.all_to_all(grad_mix_two, "ts", split_axis=1, concat_axis=0, tiled=True)
    grad_packed_patched = clip_backward(patched, attend_two, grad_patched)
    grad_packed_two = lax.all_to_all(
        grad_packed_patched, "ts", split_axis=0, concat_axis=1, tiled=True
    )
    after_time = (
        after_space.astype(jnp.float32)
        + jnp.dot(
            mixture_two.reshape(tokens, -1), output_temporal, preferred_element_type=jnp.float32
        )
    ).astype(jnp.bfloat16)
    grad_packed_two = grad_packed_two.reshape(tokens, -1)
    grad_normed_two = jnp.dot(grad_packed_two, whole_temporal.T, preferred_element_type=jnp.float32)
    grad_after = (
        cotangent_rows.astype(jnp.float32)
        + rms_norm_grad(after_space, gain_temporal, factor_two, grad_normed_two)
    ).astype(jnp.bfloat16)
    grad_mix_one = jnp.dot(grad_after, output_spatial.T, preferred_element_type=jnp.float32).astype(
        jnp.bfloat16
    )
    grad_packed_one = frame_backward(
        packed_one, attend_one, grad_mix_one.reshape(frames, places, -1)
    ).reshape(tokens, -1)
    part_spatial = lax.dot_general(
        normed_one, grad_packed_one, (((0,), (0,)), ((), ())), preferred_element_type=jnp.float32
    )
    group_spatial = lax.psum_scatter(
        part_spatial.astype(jnp.bfloat16), "dp", scatter_dimension=0, tiled=True
    )
    grad_spatial = lax.psum_scatter(group_spatial, "ts", scatter_dimension=0, tiled=True).astype(
        jnp.float32
    )
    return (after_time.reshape(frames, height, columns, -1), grad_spatial)


def solution(mesh):
    placed = (
        P(("dp", "ts"), None, None, None),
        P(),
        P(),
        P(),
        P(),
        P(("dp", "ts"), None),
        P(("dp", "ts"), None),
        P(),
        P(),
        P(("dp", "ts"), None, None, None),
    )
    return jax.shard_map(
        shards,
        mesh=mesh,
        in_specs=placed,
        out_specs=(P(("dp", "ts"), None, None, None), P(("dp", "ts"), None)),
        check_vma=False,
    )
```

profile of v0, /device:TPU:0, one launch (start us, length us, event | category | flops | bytes accessed | tf_op | source)
XLA Modules:
  0.0 313.4 jit_solution(12861886616675338777)
XLA Ops:
  7.9 2.4 collective-permute-start
  10.3 3.4 %convolution_convert_fusion.3 = bf16[320,128]{1,0:T(8,128)(2,1)S(1)} fusion(bf16[320,5120]{1,0:T(8,128)(2,1)} %bitcast.198, bf16[128,5120]{1,0:T(8,128)(2,1)} %param.18), kind=kOutput, calls=%fused_computation.72 | convolution fusion | flops 419471360 | bytes 4669440 | tf_op jit(solution)/shard_map/dot_general | solution.py:189
  13.7 0.7 copy.45
  14.4 7.2 %all-to-all-start.2 = ((bf16[2,160,128]{2,0,1:T(2,128)(2,1)}), bf16[2,160,128]{2,0,1:T(2,128)(2,1)S(1)}, u32[]{:S(2)}, u32[]{:S(2)}) async-start(bf16[2,160,128]{2,0,1:T(2,128)(2,1)} %copy.45), calls=%async_computation.2 | async-start | bytes 163840 | tf_op jit(solution)/shard_map/all_to_all | solution.py:196
  21.7 0.7 all-gather.5.cloned.1.call-update
  27.0 4.2 %fusion.4 = (f32[320]{0:T(512)S(1)}, bf16[320,5120]{1,0:T(8,128)(2,1)}) fusion(bf16[128,5120]{1,0:T(8,128)(2,1)} %param.12, f32[320,128]{1,0:T(8,128)S(1)} %convolution_add_fusion.1, bf16[320,128]{1,0:T(8,128)(2,1)S(1)} %bitcast.245, bf16[3,3,3,128,128]{4,3,2,1,0:T(8,128)(2,1)S(1)} %copy-done.4), kind=kOutput, calls=%fused_computation.15 | convolution fusion | flops 436879040 | bytes 4867328 | tf_op jit(solution)/shard_map/dot_general | solution.py:168
  31.1 44.0 %all-gather.3.cloned.1.call-done = bf16[5120,384]{1,0:T(8,128)(2,1)} async-done(((bf16[160,384]{1,0:T(8,128)(2,1)}), bf16[5120,384]{1,0:T(8,128)(2,1)}) %all-gather.3.cloned.1.call-update) | async-done | bytes 3932176 | tf_op jit(solution)/shard_map/all_gather | solution.py:159
  75.2 5.0 %convolution_convert_fusion.2 = bf16[320,384]{1,0:T(8,128)(2,1)S(1)} fusion(bf16[5120,384]{1,0:T(8,128)(2,1)} %all-gather.3.cloned.1.call-done, bf16[320,5120]{1,0:T(8,128)(2,1)} %get-tuple-element.32, f32[5120]{0:T(1024)S(1)} %copy-done.7, f32[320]{0:T(512)S(1)} %add_rsqrt_fusion.1), kind=kOutput, calls=%fused_computation.32 | convolution fusion | flops 1264967680 | bytes 7476480 | tf_op jit(solution)/shard_map/dot_general | solution.py:172
  81.0 4.9 %fusion.7 = (f32[320]{0:T(512)S(1)}, bf16[320,5120]{1,0:T(8,128)(2,1)}) fusion(bf16[320,128]{1,0:T(8,128)(2,1)S(1)} %bitcast.239, bf16[128,5120]{1,0:T(8,128)(2,1)S(1)} %copy-done, bf16[320,5120]{1,0:T(8,128)(2,1)} %get-tuple-element.32), kind=kOutput, calls=%fused_computation.18 | convolution fusion | flops 429260480 | bytes 7947520 | tf_op jit(solution)/shard_map/dot_general | solution.py:179
  85.9 51.9 %all-gather.5.cloned.1.call-done = bf16[5120,384]{1,0:T(8,128)(2,1)} async-done(((bf16[160,384]{1,0:T(8,128)(2,1)}), bf16[5120,384]{1,0:T(8,128)(2,1)}) %all-gather.5.cloned.1.call-update) | async-done | bytes 3932176 | tf_op jit(solution)/shard_map/all_gather | solution.py:160
  137.8 5.0 %fusion.22 = bf16[320,384]{1,0:T(8,128)(2,1)S(1)} fusion(bf16[5120,384]{1,0:T(8,128)(2,1)} %all-gather.5.cloned.1.call-done, bf16[320,5120]{1,0:T(8,128)(2,1)} %get-tuple-element.36, f32[5120]{0:T(1024)S(1)} %copy-done.6, f32[320]{0:T(512)S(1)} %get-tuple-element.30), kind=kOutput, calls=%fused_computation.31 | convolution fusion | flops 1264967680 | bytes 7476480 | tf_op jit(solution)/shard_map/dot_general | solution.py:184
  142.8 0.9 copy.36
  143.7 4.5 %all-to-all-start = ((bf16[2,160,384]{2,0,1:T(2,128)(2,1)}), bf16[2,160,384]{2,0,1:T(2,128)(2,1)S(1)}, u32[]{:S(2)}, u32[]{:S(2)}) async-start(bf16[2,160,384]{2,0,1:T(2,128)(2,1)} %copy.36), calls=%async_computation | async-start | bytes 491520 | tf_op jit(solution)/shard_map/all_to_all | solution.py:193
  148.3 9.6 %all-to-all-done = bf16[2,160,384]{2,0,1:T(2,128)(2,1)S(1)} async-done(((bf16[2,160,384]{2,0,1:T(2,128)(2,1)}), bf16[2,160,384]{2,0,1:T(2,128)(2,1)S(1)}, u32[]{:S(2)}, u32[]{:S(2)}) %all-to-all-start) | async-done | bytes 245792 | tf_op jit(solution)/shard_map/all_to_all | solution.py:193
  158.5 0.8 fusion.178
  160.2 14.8 %all_to_all.60 = bf16[32,10,384]{2,1,0:T(8,128)(2,1)S(1)} all-to-all(bf16[32,10,384]{2,1,0:T(8,128)(2,1)S(1)} %copy.53), channel_id=1, replica_groups=mesh['dp'=2,'ts'=16] {'ts'}, dimensions={0} | all-to-all | bytes 491520 | tf_op jit(solution)/shard_map/all_to_all | solution.py:198
  175.2 5.3 %fusion.14 = (f32[320]{0:T(512)S(1)}, f32[320,5120]{1,0:T(8,128)S(1)}) fusion(bf16[320,5120]{1,0:T(8,128)(2,1)} %get-tuple-element.36, f32[5120]{0:T(1024)S(1)} %copy-done.6, bf16[320,384]{1,0:T(8,128)(2,1)S(1)} %reshape.213, bf16[5120,384]{1,0:T(8,128)(2,1)} %all-gather.5.cloned.1.call-done), kind=kOutput, calls=%fused_computation.25 | convolution fusion | flops 1264844544 | bytes 14030080 | tf_op jit(solution)/shard_map/dot_general | solution.py:208
  180.5 2.0 fusion.32
  183.6 6.6 %convolution_convert_fusion = bf16[5120,384]{1,0:T(8,128)(2,1)} fusion(bf16[320,5120]{1,0:T(8,128)(2,1)} %get-tuple-element.32, f32[5120]{0:T(1024)S(1)} %copy-done.7, f32[320]{0:T(512)S(1)} %add_rsqrt_fusion.1, bf16[320,128]{1,0:T(8,128)(2,1)S(1)} %bitcast.252, bf16[320,128]{1,0:T(8,128)(2,1)S(1)} %bitcast.253, bf16[320,128]{1,0:T(8,128)(2,1)S(1)} %bitcast.242), kind=kOutput, calls=%fused_computation.11 | convolution fusion | flops 1267548160 | bytes 7476480 | tf_op jit(solution)/shard_map/dot_general | solution.py:219
  190.3 50.0 %reduce-scatter.3.cloned.1.call-done = bf16[2560,384]{1,0:T(8,128)(2,1)} async-done(((bf16[5120,384]{1,0:T(8,128)(2,1)}), bf16[2560,384]{1,0:T(8,128)(2,1)}) %reduce-scatter.3.cloned.1.call-update) | async-done | bytes 1966096 | tf_op jit(solution)/shard_map/reduce_scatter | solution.py:222
  240.6 13.3 %all_to_all.61 = bf16[32,10,128]{2,1,0:T(8,128)(2,1)S(1)} all-to-all(bf16[32,10,128]{2,1,0:T(8,128)(2,1)S(1)} %copy.43), channel_id=1, replica_groups=mesh['dp'=2,'ts'=16] {'ts'}, dimensions={0} | all-to-all | bytes 163840 | tf_op jit(solution)/shard_map/all_to_all | solution.py:195
  254.0 4.7 %fusion.3 = bf16[320,5120]{1,0:T(8,128)(2,1)} fusion(bf16[320,128]{1,0:T(8,128)(2,1)S(1)} %reshape.208, bf16[128,5120]{1,0:T(8,128)(2,1)S(1)} %copy-done.3, bf16[320,5120]{1,0:T(8,128)(2,1)} %get-tuple-element.36), kind=kOutput, calls=%fused_computation.13 | convolution fusion | flops 424345600 | bytes 7946240 | tf_op jit(solution)/shard_map/dot_general | solution.py:203
  258.8 46.5 %reduce-scatter.5.cloned.1.call-done = bf16[160,384]{1,0:T(8,128)(2,1)} async-done(((bf16[2560,384]{1,0:T(8,128)(2,1)}), bf16[160,384]{1,0:T(8,128)(2,1)}) %reduce-scatter.5.cloned.1.call-update) | async-done | bytes 122896 | tf_op jit(solution)/shard_map/reduce_scatter | solution.py:225
  305.2 1.6 convert_element_type.103
  (89 shorter events, 9.3 us)
Async XLA Ops:
  7.2 73.8 %copy-start = (bf16[128,5120]{1,0:T(8,128)(2,1)S(1)}, bf16[128,5120]{1,0:T(8,128)(2,1)}, u32[]{:S(2)}) copy-start(bf16[128,5120]{1,0:T(8,128)(2,1)} %param.17) | copy-start | bytes 3932164
  7.2 15.2 %copy-start.5 = (bf16[2,4,40,128]{3,2,1,0:T(8,128)(2,1)S(1)}, bf16[2,4,40,128]{3,2,1,0:T(8,128)(2,1)}, u32[]{:S(2)}) copy-start(bf16[2,4,40,128]{3,2,1,0:T(8,128)(2,1)} %param.10) | copy-start | bytes 245764
  7.2 68.0 %all-gather.3.cloned.1.call-start = ((), (), s32[]{:S(2)}) async-start(), calls=%async_computation.6 | async-start | bytes 4055040 | tf_op jit(solution)/shard_map/all_gather | solution.py:159
  7.9 14.5 %collective-permute-start = (bf16[2,4,40,128]{3,2,1,0:T(8,128)(2,1)}, bf16[2,4,40,128]{3,2,1,0:T(8,128)(2,1)S(1)}, u32[]{:S(2)}, u32[]{:S(2)}) collective-permute-start(bf16[2,4,40,128]{3,2,1,0:T(8,128)(2,1)} %param.10), channel_id=1, source_target_pairs={{0,1},{1,2},{2,3},{3,4},{4,5},{5,6},{6,7},{7,8},{8,9},{9,10},{10,1... | collective-permute-start | bytes 245768 | tf_op jit(solution)/shard_map/ppermute | solution.py:16
  10.3 12.4 %copy-start.4 = (bf16[3,3,3,128,128]{4,3,2,1,0:T(8,128)(2,1)S(1)}, bf16[3,3,3,128,128]{4,3,2,1,0:T(8,128)(2,1)}, u32[]{:S(2)}) copy-start(bf16[3,3,3,128,128]{4,3,2,1,0:T(8,128)(2,1)} %param.11) | copy-start | bytes 2654212
  14.4 129.3 %all-to-all-start.2 = ((bf16[2,160,128]{2,0,1:T(2,128)(2,1)}), bf16[2,160,128]{2,0,1:T(2,128)(2,1)S(1)}, u32[]{:S(2)}, u32[]{:S(2)}) async-start(bf16[2,160,128]{2,0,1:T(2,128)(2,1)} %copy.45), calls=%async_computation.2 | async-start | bytes 163840 | tf_op jit(solution)/shard_map/all_to_all | solution.py:196
  21.6 116.2 %all-gather.5.cloned.1.call-start = ((), (), s32[]{:S(2)}) async-start(), calls=%async_computation.7 | async-start | bytes 4055040 | tf_op jit(solution)/shard_map/all_gather | solution.py:160
  26.0 49.2 %copy-start.7 = (f32[5120]{0:T(1024)S(1)}, f32[5120]{0:T(1024)}, u32[]{:S(2)}) copy-start(f32[5120]{0:T(1024)} %param.13) | copy-start | bytes 61444
  81.0 56.8 %copy-start.6 = (f32[5120]{0:T(1024)S(1)}, f32[5120]{0:T(1024)}, u32[]{:S(2)}) copy-start(f32[5120]{0:T(1024)} %param.14) | copy-start | bytes 61444
  143.7 14.2 %all-to-all-start = ((bf16[2,160,384]{2,0,1:T(2,128)(2,1)}), bf16[2,160,384]{2,0,1:T(2,128)(2,1)S(1)}, u32[]{:S(2)}, u32[]{:S(2)}) async-start(bf16[2,160,384]{2,0,1:T(2,128)(2,1)} %copy.36), calls=%async_computation | async-start | bytes 491520 | tf_op jit(solution)/shard_map/all_to_all | solution.py:193
  148.2 92.1 %reduce-scatter.3.cloned.1.call-start = ((), (), s32[]{:S(2)}) async-start(), calls=%async_computation.8 | async-start | bytes 5898240 | tf_op jit(solution)/shard_map/reduce_scatter | solution.py:222
  175.2 5.3 %copy-start.1 = (bf16[320,5120]{1,0:T(8,128)(2,1)S(1)}, bf16[320,5120]{1,0:T(8,128)(2,1)}, u32[]{:S(2)}) copy-start(bf16[320,5120]{1,0:T(8,128)(2,1)} %get-tuple-element.36) | copy-start | bytes 9830404
  175.2 5.3 %copy-start.2 = (bf16[2,4,40,5120]{3,2,1,0:T(8,128)(2,1)S(1)}, bf16[2,4,40,5120]{3,2,1,0:T(8,128)(2,1)}, u32[]{:S(2)}) copy-start(bf16[2,4,40,5120]{3,2,1,0:T(8,128)(2,1)} %param.19) | copy-start | bytes 9830404
  190.2 63.8 %copy-start.3 = (bf16[128,5120]{1,0:T(8,128)(2,1)S(1)}, bf16[128,5120]{1,0:T(8,128)(2,1)}, u32[]{:S(2)}) copy-start(bf16[128,5120]{1,0:T(8,128)(2,1)} %param.18) | copy-start | bytes 3932164
  190.2 115.0 %reduce-scatter.5.cloned.1.call-start = ((), (), s32[]{:S(2)}) async-start(), calls=%async_computation.9 | async-start | bytes 2088960 | tf_op jit(solution)/shard_map/reduce_scatter | solution.py:225
Sparse Core Ops, SparseCore 0:
  10.9 64.2 all-gather.2
  78.1 59.6 all-gather.4
  190.4 49.8 reduce-scatter.2
  243.9 61.2 reduce-scatter.4
where the time goes:
time: 314 us; the launch traced here: 313 us
  waiting for transfers between devices  203 us (65%)
  matrix products  48.2 us (15%)
  blocking collectives  28.1 us (9%)
  starting transfers between devices  14.2 us (5%)
  between operations  14.2 us (5%)
    all_gather x1, waiting for transfers between devices, shards(): lax.all_gather(input_temporal, ('dp', 'ts'), axis=0, tiled=True)  51.9 us
    reduce_scatter x1, waiting for transfers between devices, shards(): lax.psum_scatter(part_spatial.astype(jnp.bfloat16), 'dp', scatter_dimensi...  50 us
    reduce_scatter x1, waiting for transfers between devices, shards(): lax.psum_scatter(group_spatial, 'ts', scatter_dimension=0, tiled=True)  46.5 us
    all_gather x1, waiting for transfers between devices, shards(): lax.all_gather(input_spatial, ('dp', 'ts'), axis=0, tiled=True)  44 us
    all_to_all x1, blocking collectives, shards(): lax.all_to_all(grad_packed_patched, 'ts', split_axis=0, concat_axis=1, ti...  14.8 us
    all_to_all x1, blocking collectives, shards(): lax.all_to_all(mixture_patched, 'ts', split_axis=0, concat_axis=1, tiled=...  13.3 us
    all_to_all x1, waiting for transfers between devices, shards(): lax.all_to_all(packed_two, 'ts', split_axis=1, concat_axis=0, tiled=True)  9.62 us
    all_to_all x1, starting transfers between devices, shards(): lax.all_to_all(grad_mix_two, 'ts', split_axis=1, concat_axis=0, tiled=True)  7.21 us
  transfers between devices with their start and end apart: 7, of which 5 were waited for; matrix products, arithmetic and copies ran while one was open for 11% of the time, Pallas kernels for 0%

commit v1 on v0

v1 whole, which is shorter than its diff:
```python
import jax
import jax.numpy as jnp
from jax import lax
from jax.sharding import PartitionSpec as P

FR = 16
epsilon = 1e-06
masked = -1e30
F32 = jnp.float32
BF16 = jnp.bfloat16


def mm(a, b, dims=((1,), (0,))):
    return lax.dot_general(a, b, (dims, ((), ())), preferred_element_type=F32)


def mm_t(a, b):
    return mm(a, b, ((1,), (1,)))


def t_mm(a, b):
    return mm(a, b, ((0,), (0,)))


def wide_mm(a, b):
    high = b.astype(BF16)
    low = (b - high.astype(F32)).astype(BF16)
    return mm(a, high) + mm(a, low)


def conv_local(volume, weight, count):
    frames, height, columns, channels = volume.shape
    padded = jnp.pad(volume, ((0, 0), (1, 1), (1, 1), (0, 0)))
    summed = jnp.zeros((count * height * columns, weight.shape[-1]), F32)
    for a in range(3):
        for b in range(3):
            for e in range(3):
                window = padded[2 - a : 2 - a + count, b : b + height, e : e + columns, :]
                summed = summed + mm(window.reshape(-1, channels), weight[a, b, e])
    return summed


def attend_forward(q, k, v, allowed):
    scores = mm_t(q, k) * q.shape[-1] ** -0.5
    scores = jnp.where(allowed, scores, masked)
    raised = jnp.exp(scores - jnp.max(scores, axis=-1, keepdims=True))
    attend = raised / jnp.sum(raised, axis=-1, keepdims=True)
    return mm(attend.astype(BF16), v).astype(BF16), attend


def attend_backward(q, k, v, attend, g):
    scale = q.shape[-1] ** -0.5
    grad_attend = mm_t(g, v)
    grad_values = t_mm(attend.astype(BF16), g)
    inner = jnp.sum(grad_attend * attend, axis=-1, keepdims=True)
    grad_scores = (attend * (grad_attend - inner)).astype(BF16)
    grad_q = mm(grad_scores, k) * scale
    grad_k = t_mm(grad_scores, q) * scale
    return jnp.concatenate([grad_q, grad_k, grad_values], axis=-1).astype(BF16)


def shards(
    clip_video,
    conv_weight,
    embed_weight,
    gain_spatial,
    gain_temporal,
    input_spatial,
    input_temporal,
    output_spatial,
    output_temporal,
    cotangent,
):
    frames, height, columns, channels = clip_video.shape
    rows, triple = input_spatial.shape
    head = triple // 3
    width = embed_weight.shape[-1]
    places = height * columns
    tokens = frames * places
    ts = lax.axis_size("ts")
    team = FR // frames
    share = places // team
    groups = [[c * team + i for i in range(team)] for c in range(ts // team)]
    me = lax.axis_index("dp") * ts + lax.axis_index("ts")

    route = [(i - 1, i) for i in range(1, ts)]
    prior = lax.ppermute(clip_video, "ts", route)
    volume = jnp.concatenate([prior, clip_video], axis=0)

    basis = jnp.concatenate([embed_weight, output_spatial], axis=0)
    window = lax.dynamic_slice(basis, (0, me * rows), (basis.shape[0], rows)).astype(F32)
    gain_s = lax.dynamic_slice(gain_spatial, (me * rows,), (rows,))
    gain_t = lax.dynamic_slice(gain_temporal, (me * rows,), (rows,))
    embed_rows = (window[:channels] * gain_s).astype(BF16)
    part = jnp.concatenate(
        [
            mm(embed_rows, input_spatial),
            mm((window * gain_t).astype(BF16), input_temporal),
        ],
        axis=0,
    )
    mixed = lax.psum(part.astype(BF16), ("dp", "ts"))
    map_space, map_time = mixed[:channels], mixed[channels:]
    gram = mm_t(basis, basis)
    cotangent_rows = cotangent.reshape(tokens, width)
    grad_mix_time = mm_t(cotangent_rows, output_temporal).astype(BF16)
    grad_direct = mm_t(cotangent_rows, output_spatial)

    features = jax.nn.gelu(conv_local(volume, conv_weight, frames), approximate=True).astype(BF16)
    squares = jnp.sum(
        wide_mm(features, gram[:channels, :channels]) * features.astype(F32), axis=-1, keepdims=True
    )
    factor_one = lax.rsqrt(jnp.maximum(squares, 0.0) / width + epsilon)
    packed_one = (mm(features, map_space) * factor_one).astype(BF16)
    place = jnp.arange(tokens)
    same_frame = (place[:, None] // places) == (place[None, :] // places)
    q, k, v = packed_one[:, :head], packed_one[:, head : 2 * head], packed_one[:, 2 * head :]
    mixture_one, attend_one = attend_forward(q, k, v, same_frame)
    joint = jnp.concatenate([features, mixture_one], axis=-1)
    spread = wide_mm(joint, gram)
    squares = jnp.sum(spread * joint.astype(F32), axis=-1, keepdims=True)
    factor_two = lax.rsqrt(jnp.maximum(squares, 0.0) / width + epsilon)
    packed_two = (mm(joint, map_time) * factor_two).astype(BF16)

    sent = jnp.concatenate([packed_two, grad_mix_time], axis=-1).reshape(frames, places, 4 * head)
    got = lax.all_to_all(
        sent, "ts", split_axis=1, concat_axis=0, tiled=True, axis_index_groups=groups
    ).reshape(FR * share, 4 * head)
    spot = jnp.arange(FR * share)
    allowed = ((spot[:, None] % share) == (spot[None, :] % share)) & (
        spot[:, None] >= spot[None, :]
    )
    tq, tk, tv, tg = (got[:, i * head : (i + 1) * head] for i in range(4))
    mixture_two, attend_two = attend_forward(tq, tk, tv, allowed)
    grad_two = attend_backward(tq, tk, tv, attend_two, tg)
    back = jnp.concatenate([mixture_two, grad_two], axis=-1).reshape(FR, share, 4 * head)
    home = lax.all_to_all(
        back, "ts", split_axis=0, concat_axis=1, tiled=True, axis_index_groups=groups
    ).reshape(tokens, 4 * head)
    mixture_two, grad_two = home[:, :head], home[:, head:]

    output = mm(
        jnp.concatenate([joint, mixture_two], axis=-1),
        jnp.concatenate([basis, output_temporal], axis=0),
    ).astype(BF16)

    inner = jnp.sum(grad_two.astype(F32) * packed_two.astype(F32), axis=-1, keepdims=True)
    grad_mix_one = (
        grad_direct
        + factor_two * mm_t(grad_two, map_time[channels:])
        - (factor_two**2 * inner / width) * spread[:, channels:]
    ).astype(BF16)
    grad_one = attend_backward(q, k, v, attend_one, grad_mix_one)
    scaled = (features.astype(F32) * factor_one).astype(BF16)
    core = lax.psum(t_mm(scaled, grad_one).astype(BF16), ("dp", "ts"))
    return output.reshape(frames, height, columns, width), t_mm(embed_rows, core)


def solution(mesh):
    placed = (
        P(("dp", "ts"), None, None, None),
        P(),
        P(),
        P(),
        P(),
        P(("dp", "ts"), None),
        P(("dp", "ts"), None),
        P(),
        P(),
        P(("dp", "ts"), None, None, None),
    )
    return jax.shard_map(
        shards,
        mesh=mesh,
        in_specs=placed,
        out_specs=(P(("dp", "ts"), None, None, None), P(("dp", "ts"), None)),
        check_vma=False,
    )
```

time: 314 us -> 331 us (1.054)
  waiting for transfers between devices: 203 us -> 242 us
  matrix products: 48.2 us -> 31.3 us
  blocking collectives: 28.1 us -> 11.4 us
  local copies, waits for them, and re-layouts: 2.6 us -> 18.4 us
  starting transfers between devices: 14.2 us -> 8.29 us
    psum x0 -> x2, waiting for transfers between devices: none -> 235 us  [the longest x1 119 us: shards(): mixed = lax.psum(part.astype(BF16), ('dp', 'ts'))]
    reduce_scatter x2 -> x0, waiting for transfers between devices: 96.5 us -> none  [the longest x1 50 us: shards(): lax.psum_scatter(part_spatial.astype(jnp.bfloat16), 'dp', scatter_dimensi...]
    all_gather x2 -> x0, waiting for transfers between devices: 96 us -> none  [the longest x1 51.9 us: shards(): lax.all_gather(input_temporal, ('dp', 'ts'), axis=0, tiled=True)]
    all_to_all x2 -> x1, blocking collectives: 28.1 us -> 11.4 us  [shards(): lax.all_to_all(back, 'ts', split_axis=0, concat_axis=1, tiled=True, axis_...]
    dot_general x46 -> x54, matrix products: 47.9 us -> 31.3 us  [mm(): return lax.dot_general(a, b, (dims, ((), ())), preferred_element_type=F32)]
    all_to_all x2 -> x1, starting transfers between devices: 11.7 us -> 5.55 us  [shards(): lax.all_to_all(sent, 'ts', split_axis=1, concat_axis=0, tiled=True, axis_...]
    unnamed x16 -> x32, local copies, waits for them, and re-layouts: 0.04 us -> 4.69 us
    reshape x6 -> x4, local copies, waits for them, and re-layouts: 1.83 us -> 6.4 us  [the longest x1 1.79 us: shards(): got = lax.all_to_all(sent, 'ts', split_axis=1, concat_axis=0, tiled=True,...]
  transfers between devices with their start and end apart: 7 -> 4, of which waited for: 5 -> 3; matrix products, arithmetic and copies ran while one was open for 11% -> 8% of each run, Pallas kernels for 0% -> 0%
where the time goes in v1:
time: 331 us; the launch traced here: 330 us
  waiting for transfers between devices  242 us (73%)
  matrix products  31.3 us (9%)
  local copies, waits for them, and re-layouts  18.4 us (6%)
  between operations  14.5 us (4%)
  blocking collectives  11.4 us (3%)
  starting transfers between devices  8.29 us (3%)
  other arithmetic  4.29 us (1%)
    psum x1, waiting for transfers between devices, shards(): mixed = lax.psum(part.astype(BF16), ('dp', 'ts'))  119 us
    psum x1, waiting for transfers between devices, shards(): core = lax.psum(t_mm(scaled, grad_one).astype(BF16), ('dp', 'ts'))  116 us
    dot_general x54, matrix products, mm(): return lax.dot_general(a, b, (dims, ((), ())), preferred_element_type=F32)  31.3 us
    all_to_all x1, blocking collectives, shards(): lax.all_to_all(back, 'ts', split_axis=0, concat_axis=1, tiled=True, axis_...  11.4 us
    all_to_all x1, waiting for transfers between devices, shards(): lax.all_to_all(sent, 'ts', split_axis=1, concat_axis=0, tiled=True, axis_...  6.8 us
  transfers between devices with their start and end apart: 4, of which 3 were waited for; matrix products, arithmetic and copies ran while one was open for 8% of the time, Pallas kernels for 0%

profile of v1, /device:TPU:0, one launch (start us, length us, event | category | flops | bytes accessed | tf_op | source)
XLA Modules:
  0.0 330.1 jit_solution(1640951019662262618)
XLA Ops:
  7.2 2.7 collective-permute-start
  9.9 2.5 constant_dynamic-update-slice_fusion.3
  12.4 2.5 constant_dynamic-update-slice_fusion.2
  17.5 1.2 convolution_convert_fusion.1
  18.7 1.1 convolution_convert_fusion.3
  20.6 3.5 %fusion.148 = f32[256,256]{1,0:T(8,128)S(1)} fusion(bf16[256,5120]{1,0:T(8,128)(2,1)} %constant_dynamic-update-slice_fusion.2), kind=kOutput, calls=%fused_computation.247 | convolution fusion | flops 671088640 | bytes 2883584 | tf_op jit(solution)/shard_map/dot_general | solution.py:14
  31.2 119.2 %all-reduce.4.cloned.1.call-done = bf16[384,384]{1,0:T(8,128)(2,1)} async-done(((bf16[384,384]{1,0:T(8,128)(2,1)}), bf16[384,384]{1,0:T(8,128)(2,1)}) %all-reduce.4.cloned.1.call-update) | async-done | bytes 294928 | tf_op jit(solution)/shard_map/psum | solution.py:102
  150.4 1.1 fusion.7
  155.1 1.0 copy.12
  156.1 5.6 %all-to-all-start = ((bf16[2,160,512]{2,0,1:T(2,128)(2,1)}), bf16[2,160,512]{2,0,1:T(2,128)(2,1)}, u32[]{:S(2)}, u32[]{:S(2)}) async-start(bf16[2,160,512]{2,0,1:T(2,128)(2,1)} %copy.12), calls=%async_computation | async-start | bytes 655360 | tf_op jit(solution)/shard_map/all_to_all | solution.py:126
  161.7 6.8 %all-to-all-done = bf16[2,160,512]{2,0,1:T(2,128)(2,1)} async-done(((bf16[2,160,512]{2,0,1:T(2,128)(2,1)}), bf16[2,160,512]{2,0,1:T(2,128)(2,1)}, u32[]{:S(2)}, u32[]{:S(2)}) %all-to-all-start) | async-done | bytes 327712 | tf_op jit(solution)/shard_map/all_to_all | solution.py:126
  168.5 1.8 copy.13
  170.3 1.8 reshape.248
  172.1 1.2 fusion.147
  173.4 1.2 convolution_convert_fusion.7
  176.5 1.8 reshape.249
  178.3 11.4 %all_to_all.30 = bf16[16,20,512]{2,1,0:T(8,128)(2,1)S(1)} all-to-all(bf16[16,20,512]{2,1,0:T(8,128)(2,1)} %reshape.249), channel_id=1, replica_groups={{0,1,2,3,4,5,6,7},{8,9,10,11,12,13,14,15},{16,17,18,19,20,21,22,23},{24..., dimensions={0} | all-to-all | bytes 655360 | tf_op jit(solution)/shard_map/all_to_all | solution.py:137
  190.9 1.8 reshape.250
  192.7 1.2 multiply_reduce_fusion.1
  193.9 1.3 convolution_multiply_fusion.6
  195.2 2.4 fusion.16
  199.8 5.7 %convolution_convert_fusion = bf16[320,5120]{1,0:T(8,128)(2,1)} fusion(bf16[128,5120]{1,0:T(8,128)(2,1)} %param.18, bf16[128,5120]{1,0:T(8,128)(2,1)} %param.17, bf16[128,5120]{1,0:T(8,128)(2,1)} %param.12, bf16[320,128]{1,0:T(8,128)(2,1)S(1)} %slice-done, bf16[320,128]{1,0:T(8,128)(2,1)S(1)} %convolution_convert_fusion.8, bf16[320,128]{1,0:T(8,128)(2,1)S(1)} %fusion.43), kind=kOutput, calls=%fused_computation | convolution fusion | flops 1272463360 | bytes 7454720 | tf_op jit(solution)/shard_map/dot_general | solution.py:14
  205.5 115.9 %all-reduce.6.cloned.1.call-done = bf16[128,384]{1,0:T(8,128)(2,1)} async-done(((bf16[128,384]{1,0:T(8,128)(2,1)}), bf16[128,384]{1,0:T(8,128)(2,1)}) %all-reduce.6.cloned.1.call-update) | async-done | bytes 98320 | tf_op jit(solution)/shard_map/psum | solution.py:155
  321.4 1.9 fusion.129
  (102 shorter events, 19.2 us)
Async XLA Ops:
  7.2 16.9 %copy-start = (bf16[2,4,40,5120]{3,2,1,0:T(8,128)(2,1)S(1)}, bf16[2,4,40,5120]{3,2,1,0:T(8,128)(2,1)}, u32[]{:S(2)}) copy-start(bf16[2,4,40,5120]{3,2,1,0:T(8,128)(2,1)} %param.19) | copy-start | bytes 9830404
  7.2 143.2 %all-reduce.4.cloned.1.call-start = ((), (), s32[]{:S(2)}) async-start(), calls=%async_computation.2 | async-start | bytes 589824 | tf_op jit(solution)/shard_map/psum | solution.py:102
  7.2 18.0 %collective-permute-start = (bf16[2,4,40,128]{3,2,1,0:T(8,128)(2,1)}, bf16[2,4,40,128]{3,2,1,0:T(8,128)(2,1)S(1)}, u32[]{:S(2)}, u32[]{:S(2)}) collective-permute-start(bf16[2,4,40,128]{3,2,1,0:T(8,128)(2,1)} %param.10), channel_id=1, source_target_pairs={{0,1},{1,2},{2,3},{3,4},{4,5},{5,6},{6,7},{7,8},{8,9},{9,10},{10,1... | collective-permute-start | bytes 245768 | tf_op jit(solution)/shard_map/ppermute | solution.py:87
  9.9 7.6 %copy-start.13 = (bf16[160,384]{1,0:T(8,128)(2,1)S(1)}, bf16[160,384]{1,0:T(8,128)(2,1)}, u32[]{:S(2)}) copy-start(bf16[160,384]{1,0:T(8,128)(2,1)} %param.16) | copy-start | bytes 368644
  15.9 2.8 copy-start.6
  20.6 3.6 %copy-start.5 = (bf16[128,5120]{1,0:T(8,128)(2,1)S(1)}, bf16[128,5120]{1,0:T(8,128)(2,1)}, u32[]{:S(2)}) copy-start(bf16[128,5120]{1,0:T(8,128)(2,1)} %param.18) | copy-start | bytes 3932164
  24.1 6.8 %copy-start.3 = (f32[256,256]{1,0:T(8,128)}, f32[256,256]{1,0:T(8,128)S(1)}, u32[]{:S(2)}) copy-start(f32[256,256]{1,0:T(8,128)S(1)} %fusion.148) | copy-start | bytes 786436
  24.1 1.1 copy-start.12
  25.2 1.2 copy-start.8
  150.4 2.5 copy-start.4
  151.6 1.3 copy-start.10
  151.6 2.5 copy-start.14
  151.8 0.8 copy-start.1
  154.4 0.7 copy-start.7
  156.1 12.4 %all-to-all-start = ((bf16[2,160,512]{2,0,1:T(2,128)(2,1)}), bf16[2,160,512]{2,0,1:T(2,128)(2,1)}, u32[]{:S(2)}, u32[]{:S(2)}) async-start(bf16[2,160,512]{2,0,1:T(2,128)(2,1)} %copy.12), calls=%async_computation | async-start | bytes 655360 | tf_op jit(solution)/shard_map/all_to_all | solution.py:126
  161.7 159.7 %all-reduce.6.cloned.1.call-start = ((), (), s32[]{:S(2)}) async-start(), calls=%async_computation.3 | async-start | bytes 196608 | tf_op jit(solution)/shard_map/psum | solution.py:155
  172.1 2.5 copy-start.9
  195.2 2.4 copy-start.2
  195.2 2.4 copy-start.11
  197.9 1.9 slice-start
Sparse Core Ops, SparseCore 0:
  20.7 129.6 all-reduce.3
  200.0 121.3 all-reduce.5

commit v2 on v1

v2 whole, which is shorter than its diff:
```python
import functools

import jax
import jax.numpy as jnp
import numpy as np
from jax import lax
from jax.experimental import pallas as pl
from jax.experimental.pallas import tpu as pltpu
from jax.sharding import PartitionSpec as P

FR = 16
REDUCERS = 24
epsilon = 1e-06
masked = -1e30
F32 = jnp.float32
BF16 = jnp.bfloat16
MESH = pl.DeviceIdType.MESH


def mm(a, b, dims=((1,), (0,))):
    return lax.dot_general(a, b, (dims, ((), ())), preferred_element_type=F32)


def mm_t(a, b):
    return mm(a, b, ((1,), (1,)))


def t_mm(a, b):
    return mm(a, b, ((0,), (0,)))


def wide_mm(a, b):
    high = b.astype(BF16)
    low = (b - high.astype(F32)).astype(BF16)
    return mm(a, high) + mm(a, low)


def attend_forward(q, k, v, bias):
    scores = mm_t(q, k) * q.shape[-1] ** -0.5 + bias.astype(F32)
    raised = jnp.exp(scores - jnp.max(scores, axis=-1, keepdims=True))
    attend = raised / jnp.sum(raised, axis=-1, keepdims=True)
    return mm(attend.astype(BF16), v).astype(BF16), attend


def attend_backward(q, k, v, attend, g):
    scale = q.shape[-1] ** -0.5
    grad_attend = mm_t(g, v)
    grad_values = t_mm(attend.astype(BF16), g)
    inner = jnp.sum(grad_attend * attend, axis=-1, keepdims=True)
    grad_scores = (attend * (grad_attend - inner)).astype(BF16)
    grad_q = mm(grad_scores, k) * scale
    grad_k = t_mm(grad_scores, q) * scale
    return jnp.concatenate([grad_q, grad_k, grad_values], axis=-1).astype(BF16)


def stacked(block):
    third = block.shape[1] // 3
    return jnp.concatenate([block[:, i * third : (i + 1) * third] for i in range(3)], axis=0)


def unstacked(block):
    third = block.shape[0] // 3
    return jnp.concatenate([block[i * third : (i + 1) * third] for i in range(3)], axis=1)


def moved(block, distance):
    if distance == 0:
        return block
    return pltpu.roll(block, distance % block.shape[0], 0)


def whole_kernel(
    dims,
    video_hbm, conv_hbm, embed_hbm, gain_s_hbm, gain_t_hbm, in_s_hbm, in_t_hbm, out_s_hbm,
    out_t_hbm, cot_hbm, perm_hbm, frame_bias_hbm, clip_bias_hbm, edge_hbm,
    result, grad_result,
    video, prior, taps, basis, gain_s, gain_t, in_s, in_t, cot, perm, frame_bias, clip_bias, edge,
    part_a, part_b, part_c, land_a, land_b, land_c, full_a, full_b, full_c,
    sent, got, back, home, gram, direct,
    local_sem, send_sem, recv_sem,
):
    n_dp, n_ts, frames, places, columns, team, share, pad, rows, window = dims
    n = n_dp * n_ts
    head = 128
    width = basis.shape[1]
    tokens = frames * places
    dp, ts = lax.axis_index("dp"), lax.axis_index("ts")
    me = dp * n_ts + ts

    loads = [
        (in_s_hbm, in_s), (in_t_hbm, in_t), (gain_s_hbm, gain_s), (gain_t_hbm, gain_t),
        (embed_hbm, basis.at[0:head]), (out_s_hbm, basis.at[head : 2 * head]),
        (video_hbm, video), (edge_hbm, edge), (conv_hbm, taps), (frame_bias_hbm, frame_bias),
        (perm_hbm, perm), (out_t_hbm, basis.at[2 * head : 3 * head]), (cot_hbm, cot),
        (clip_bias_hbm, clip_bias),
    ]
    copies = [pltpu.make_async_copy(s, d, local_sem.at[i]) for i, (s, d) in enumerate(loads)]
    for copy in copies:
        copy.start()

    barrier = pltpu.get_barrier_semaphore()

    def greet(i, carry):
        dev = lax.rem(me + i, n)
        pl.semaphore_signal(
            barrier, inc=1, device_id=(dev // n_ts, lax.rem(dev, n_ts)), device_id_type=MESH
        )
        return carry

    lax.fori_loop(1, n, greet, 0)

    def remote(src, dst, index, dev):
        return pltpu.make_async_remote_copy(
            src_ref=src, dst_ref=dst, send_sem=send_sem.at[index], recv_sem=recv_sem.at[index],
            device_id=(dev // n_ts, lax.rem(dev, n_ts)), device_id_type=MESH,
        )

    def settle(ref, count, sem):
        piece = ref.at[pl.ds(0, count)]
        pltpu.make_async_copy(piece, piece, sem).wait()

    reducing = lax.rem(me, 4) != 3
    inside = me < REDUCERS // 3 * 4
    leads = jnp.logical_and(reducing, inside)
    mine = (me // 4) * 3 + lax.rem(me, 4)

    def scatter(part, land, index):
        def step(i, carry):
            r = lax.rem(me + i, REDUCERS)
            dev = r + r // 3

            @pl.when(dev != me)
            def _():
                remote(part.at[r], land.at[me], index, dev).start()

            return carry

        lax.fori_loop(0, REDUCERS, step, 0)

    def gather(part, land, full, index):
        @pl.when(leads)
        def _():
            land[pl.ds(me, 1)] = part[pl.ds(mine, 1)]
            settle(land, n - 1, recv_sem.at[index])
            total = jnp.sum(land[...].astype(F32), axis=0, keepdims=True)
            full[pl.ds(mine, 1)] = total.astype(BF16)

            def step(i, carry):
                dev = lax.rem(me + i, n)
                remote(full.at[mine], full.at[mine], index + 1, dev).start()
                return carry

            lax.fori_loop(1, n, step, 0)

    def collect(part, land, full, index):
        @pl.when(leads)
        def _():
            settle(full, REDUCERS - 1, recv_sem.at[index + 1])
            settle(part, REDUCERS - 1, send_sem.at[index])
            settle(land, n - 1, send_sem.at[index + 1])

        @pl.when(jnp.logical_not(leads))
        def _():
            settle(full, REDUCERS, recv_sem.at[index + 1])
            settle(part, REDUCERS, send_sem.at[index])

        return unstacked(full[...].reshape(-1, head))

    for copy in copies[:6]:
        copy.wait()
    first = me * rows
    start = pl.multiple_of(first // 128 * 128, 128)
    if (n * rows - rows) // 128 * 128 + window > width:
        limit = width - window
        start = pl.multiple_of(jnp.where(start > limit, limit, start), 128)
    shift = first - start
    place = lax.broadcasted_iota(jnp.int32, (window, rows), 0)
    source = lax.broadcasted_iota(jnp.int32, (window, rows), 1)
    chosen = jnp.where(place == source + shift, 1.0, 0.0).astype(BF16)
    spread_s = mm(chosen, in_s[...]).astype(BF16)
    spread_t = mm(chosen, in_t[...]).astype(BF16)
    span = basis[0 : 2 * head, pl.ds(start, window)].astype(F32)
    span_s = (span[:head] * gain_s[:, pl.ds(start, window)]).astype(BF16)
    span_t = (span * gain_t[:, pl.ds(start, window)]).astype(BF16)
    part_a[...] = stacked(mm(span_s, spread_s)).astype(BF16).reshape(part_a.shape)
    part_b[...] = stacked(mm(span_t, spread_t)).astype(BF16).reshape(part_b.shape)
    copies[6].wait()

    pl.semaphore_wait(barrier, n - 1)
    halo = remote(video.at[pl.ds(frames - 2, 2)], prior, 0, me + 1)
    halo_in = remote(video.at[pl.ds(frames - 2, 2)], prior, 0, me)

    @pl.when(ts < n_ts - 1)
    def _():
        halo.start()

    scatter(part_a, land_a, 1)
    scatter(part_b, land_b, 3)
    embed_rows = mm(span_s, chosen).astype(BF16)

    @pl.when(ts == 0)
    def _():
        prior[...] = jnp.zeros_like(prior)

    @pl.when(ts > 0)
    def _():
        halo_in.wait_recv()

    for copy in copies[7:11]:
        copy.wait()
    volume = jnp.concatenate([prior[...], video[...]], axis=0)
    deep = jnp.concatenate(
        [volume[2 - a : 2 - a + frames].reshape(tokens, head) for a in range(3)], axis=1
    )
    edges = edge[...].astype(F32)
    by_col = [None, None, None]
    for b in range(3):
        weight = jnp.concatenate(
            [jnp.concatenate([taps[a, b, e] for a in range(3)], axis=0) for e in range(3)], axis=1
        )
        product = mm(deep, weight)
        product = moved(product, -(b - 1) * columns)
        if b == 0:
            product = product * edges[:, 0:1]
        if b == 2:
            product = product * edges[:, 1:2]
        for e in range(3):
            piece = product[:, e * head : (e + 1) * head]
            by_col[e] = piece if by_col[e] is None else by_col[e] + piece
    summed = (
        by_col[1] + moved(by_col[0], 1) * edges[:, 2:3] + moved(by_col[2], -1) * edges[:, 3:4]
    )
    features = jax.nn.gelu(summed, approximate=True).astype(BF16)

    gather(part_a, land_a, full_a, 1)

    for copy in copies[11:]:
        copy.wait()
    chunk = width // 5
    gram[...] = jnp.zeros_like(gram)
    direct[...] = jnp.zeros_like(direct)

    def slab(i, carry):
        cols = pl.ds(pl.multiple_of(i * chunk, 128), chunk)
        pair = basis[0 : 2 * head, cols]
        gram[...] += mm_t(pair, pair)
        direct[...] += mm_t(cot[:, cols], basis[head : 3 * head, cols])
        return carry

    lax.fori_loop(0, 5, slab, 0)
    grad_mix_time = direct[:, head:].astype(BF16)
    grams = gram[...]

    gather(part_b, land_b, full_b, 3)

    squares = jnp.sum(
        wide_mm(features, grams[:head, :head]) * features.astype(F32), axis=-1, keepdims=True
    )
    factor_one = lax.rsqrt(jnp.maximum(squares, 0.0) / width + epsilon)
    map_space = collect(part_a, land_a, full_a, 1)
    packed_one = (mm(features, map_space) * factor_one).astype(BF16)
    q, k, v = packed_one[:, :head], packed_one[:, head : 2 * head], packed_one[:, 2 * head :]
    mixture_one, attend_one = attend_forward(q, k, v, frame_bias[...])
    joint = jnp.concatenate([features, mixture_one], axis=-1)
    spread = wide_mm(joint, grams)
    squares = jnp.sum(spread * joint.astype(F32), axis=-1, keepdims=True)
    factor_two = lax.rsqrt(jnp.maximum(squares, 0.0) / width + epsilon)
    map_time = collect(part_b, land_b, full_b, 3)
    packed_two = (mm(joint, map_time) * factor_two).astype(BF16)

    seat = lax.rem(ts, team)
    base = me - seat
    order = perm[...]

    def swap(source_ref, target_ref, index):
        def step(i, carry):
            other = lax.rem(seat + i, team)
            remote(source_ref.at[other], target_ref.at[seat], index, base + other).start()
            return carry

        lax.fori_loop(1, team, step, 0)
        target_ref[pl.ds(seat, 1)] = source_ref[pl.ds(seat, 1)]

    sent[...] = (
        mm(order, jnp.concatenate([packed_two, grad_mix_time], axis=-1))
        .astype(BF16)
        .reshape(sent.shape)
    )
    swap(sent, got, 5)
    settle(got, team - 1, recv_sem.at[5])
    arrived = got[...].reshape(team * pad, 4 * head)
    tq, tk, tv, tg = (arrived[:, i * head : (i + 1) * head] for i in range(4))
    mixture_two, attend_two = attend_forward(tq, tk, tv, clip_bias[...])
    grad_two = attend_backward(tq, tk, tv, attend_two, tg)
    back[...] = jnp.concatenate([mixture_two, grad_two], axis=-1).reshape(back.shape)
    swap(back, home, 6)
    settle(home, team - 1, recv_sem.at[6])
    returned = t_mm(order, home[...].reshape(team * pad, 4 * head)).astype(BF16)
    mixture_two, grad_two = returned[:, :head], returned[:, head:]

    inner = jnp.sum(grad_two.astype(F32) * packed_two.astype(F32), axis=-1, keepdims=True)
    grad_mix_one = (
        direct[:, :head]
        + factor_two * mm_t(grad_two, map_time[head:])
        - (factor_two * factor_two * inner / width) * spread[:, head:]
    ).astype(BF16)
    grad_one = attend_backward(q, k, v, attend_one, grad_mix_one)
    scaled = (features.astype(F32) * factor_one).astype(BF16)
    part_c[...] = stacked(t_mm(scaled, grad_one)).astype(BF16).reshape(part_c.shape)
    scatter(part_c, land_c, 7)

    triple = jnp.concatenate([joint, mixture_two], axis=-1)

    def write(i, carry):
        cols = pl.ds(pl.multiple_of(i * chunk, 128), chunk)
        result[:, cols] = mm(triple, basis[:, cols]).astype(BF16)
        return carry

    lax.fori_loop(0, 2, write, 0)
    gather(part_c, land_c, full_c, 7)
    lax.fori_loop(2, 5, write, 0)
    total = collect(part_c, land_c, full_c, 7)
    grad_result[...] = t_mm(embed_rows, total)

    @pl.when(ts < n_ts - 1)
    def _():
        halo.wait_send()

    settle(sent, team - 1, send_sem.at[5])
    settle(back, team - 1, send_sem.at[6])


def shards(
    clip_video, conv_weight, embed_weight, gain_spatial, gain_temporal, input_spatial,
    input_temporal, output_spatial, output_temporal, cotangent,
):
    frames, height, columns, channels = clip_video.shape
    rows, triple = input_spatial.shape
    head = triple // 3
    width = embed_weight.shape[-1]
    places = height * columns
    tokens = frames * places
    n_dp, n_ts = lax.axis_size("dp"), lax.axis_size("ts")
    n = n_dp * n_ts
    team = FR // frames
    share = places // team
    pad = -(-frames * share // 16) * 16
    reach = max(i * rows % 128 + rows for i in range(n))
    window = -(-reach // 128) * 128

    token = np.arange(tokens)
    frame, spot = token // places, token % places
    slot = spot // share * pad + frame * share + spot % share
    perm = np.zeros((team * pad, tokens), np.float32)
    perm[slot, token] = 1.0
    frame_bias = np.where(frame[:, None] == frame[None, :], 0.0, masked)
    seat = np.arange(team * pad)
    local = seat % pad
    when = seat // pad * frames + local // share
    valid = local < frames * share
    allowed = (
        (local[:, None] % share == local[None, :] % share)
        & (when[:, None] >= when[None, :])
        & valid[:, None]
        & valid[None, :]
    )
    clip_bias = np.where(allowed, 0.0, masked)
    edge = np.zeros((tokens, 128), np.float32)
    edge[:, 0] = spot // columns >= 1
    edge[:, 1] = spot // columns < height - 1
    edge[:, 2] = spot % columns >= 1
    edge[:, 3] = spot % columns < columns - 1

    dims = (n_dp, n_ts, frames, places, columns, team, share, pad, rows, window)
    any_space = pl.BlockSpec(memory_space=pl.ANY)
    vmem = pl.BlockSpec(memory_space=pltpu.VMEM)
    buffer = lambda *shape: pltpu.VMEM(shape, BF16)
    wide = lambda *shape: pltpu.VMEM(shape, F32)
    output, grad = pl.pallas_call(
        functools.partial(whole_kernel, dims),
        out_shape=(
            jax.ShapeDtypeStruct((tokens, width), BF16),
            jax.ShapeDtypeStruct((rows, triple), F32),
        ),
        in_specs=[any_space] * 14,
        out_specs=(vmem, vmem),
        scratch_shapes=[
            buffer(frames, places, channels), buffer(2, places, channels),
            buffer(*conv_weight.shape), buffer(3 * head, width), wide(1, width), wide(1, width),
            buffer(rows, triple), buffer(rows, triple), buffer(tokens, width),
            buffer(team * pad, tokens), buffer(tokens, tokens), buffer(team * pad, team * pad),
            buffer(tokens, 128),
            buffer(REDUCERS, 16, 128), buffer(REDUCERS, 32, 128), buffer(REDUCERS, 16, 128),
            buffer(n, 16, 128), buffer(n, 32, 128), buffer(n, 16, 128),
            buffer(REDUCERS, 16, 128), buffer(REDUCERS, 32, 128), buffer(REDUCERS, 16, 128),
            buffer(team, pad, 4 * head), buffer(team, pad, 4 * head),
            buffer(team, pad, 4 * head), buffer(team, pad, 4 * head),
            wide(2 * head, 2 * head), wide(tokens, 2 * head),
            pltpu.SemaphoreType.DMA((14,)), pltpu.SemaphoreType.DMA((9,)),
            pltpu.SemaphoreType.DMA((9,)),
        ],
        compiler_params=pltpu.CompilerParams(
            collective_id=0, has_side_effects=True, vmem_limit_bytes=56 * 1024 * 1024
        ),
    )(
        clip_video.reshape(frames, places, channels),
        conv_weight,
        embed_weight,
        gain_spatial.reshape(1, width),
        gain_temporal.reshape(1, width),
        input_spatial,
        input_temporal,
        output_spatial,
        output_temporal,
        cotangent.reshape(tokens, width),
        jnp.asarray(perm, BF16),
        jnp.asarray(frame_bias, BF16),
        jnp.asarray(clip_bias, BF16),
        jnp.asarray(edge, BF16),
    )
    return output.reshape(frames, height, columns, width), grad


def solution(mesh):
    placed = (
        P(("dp", "ts"), None, None, None), P(), P(), P(), P(), P(("dp", "ts"), None),
        P(("dp", "ts"), None), P(), P(), P(("dp", "ts"), None, None, None),
    )
    return jax.shard_map(
        shards,
        mesh=mesh,
        in_specs=placed,
        out_specs=(P(("dp", "ts"), None, None, None), P(("dp", "ts"), None)),
        check_vma=False,
    )
```

time: 331 us -> 57.4 us (0.17)
  waiting for transfers between devices: 242 us -> 0 us
  Pallas kernels: 0 us -> 52 us
  matrix products: 31.3 us -> 0 us
  between operations: 14.5 us -> 0.65 us
  local copies, waits for them, and re-layouts: 18.4 us -> 4.58 us
  blocking collectives: 11.4 us -> 0 us
  starting transfers between devices: 8.29 us -> 0 us
  other arithmetic: 4.29 us -> 0 us
    psum x2 -> x0, waiting for transfers between devices: 235 us -> none  [the longest x1 119 us: shards(): mixed = lax.psum(part.astype(BF16), ('dp', 'ts'))]
    pallas_call x0 -> x1, Pallas kernels: none -> 52 us  [shards(): pl.pallas_call(functools.partial(whole_kernel, dims), out_shape=(jax.Shap...]
    dot_general x54 -> x0, matrix products: 31.3 us -> none  [mm(): return lax.dot_general(a, b, (dims, ((), ())), preferred_element_type=F32)]
    all_to_all x1 -> x0, blocking collectives: 11.4 us -> none  [shards(): lax.all_to_all(back, 'ts', split_axis=0, concat_axis=1, tiled=True, axis_...]
    all_to_all x1 -> x0, waiting for transfers between devices: 6.8 us -> none  [shards(): lax.all_to_all(sent, 'ts', split_axis=1, concat_axis=0, tiled=True, axis_...]
    reshape x4 -> x0, local copies, waits for them, and re-layouts: 6.4 us -> none  [the longest x1 1.79 us: shards(): got = lax.all_to_all(sent, 'ts', split_axis=1, concat_axis=0, tiled=True,...]
    all_to_all x1 -> x0, starting transfers between devices: 5.55 us -> none  [shards(): lax.all_to_all(sent, 'ts', split_axis=1, concat_axis=0, tiled=True, axis_...]
  transfers between devices with their start and end apart: 4 -> 0, of which waited for: 3 -> 0; matrix products, arithmetic and copies ran while one was open for 8% -> 0% of each run, Pallas kernels for 0% -> 0%
where the time goes in v2:
time: 57.4 us; the launch traced here: 57.3 us
  Pallas kernels  52 us (91%)
  local copies, waits for them, and re-layouts  4.58 us (8%)
  between operations  0.65 us (1%)
    pallas_call x1, Pallas kernels, shards(): pl.pallas_call(functools.partial(whole_kernel, dims), out_shape=(jax.Shap...  52 us
    unnamed x4, local copies, waits for them, and re-layouts  4.58 us

profile of v2, /device:TPU:0, one launch (start us, length us, event | category | flops | bytes accessed | tf_op | source)
XLA Modules:
  0.0 57.3 jit_solution(7875322641833153663)
XLA Ops:
  0.6 52.0 %shard_map.149 = (bf16[320,5120]{1,0:T(8,128)(2,1)}, f32[160,384]{1,0:T(8,128)}) custom-call(bf16[2,160,128]{2,1,0:T(8,128)(2,1)} %bitcast.7, bf16[3,3,3,128,128]{4,3,2,1,0:T(8,128)(2,1)} %conv_hbm.1, bf16[128,5120]{1,0:T(8,128)(2,1)} %embed_hbm.1, f32[1,5120]{1,0:T(1,128)} %bitcast.8, f32[1,5120]{1,0:T(1,128)} %bitcast.9, bf16[160,384]{1,0:T(8,128)(2,1)} %in_s_hbm.1, ...), custom_call_target="tpu_custom_call" | custom-call | tf_op jit(solution)/shard_map/pallas_call | solution.py:379
  52.7 0.0 copy-start
  52.7 3.9 %copy.18 = bf16[2,4,40,5120]{3,2,1,0:T(8,128)(2,1)} copy(bf16[2,4,40,5120]{3,2,1,0:T(8,128)(2,1)} %bitcast.5) | data formatting | bytes 6553600
  56.6 0.0 copy-done
  56.6 0.7 %copy.19 = f32[160,384]{1,0:T(8,128)} copy(f32[160,384]{1,0:T(8,128)S(1)} %copy-done) | data formatting | bytes 491520
Async XLA Ops:
  52.7 3.9 %copy-start = (f32[160,384]{1,0:T(8,128)S(1)}, f32[160,384]{1,0:T(8,128)}, u32[]{:S(2)}) copy-start(f32[160,384]{1,0:T(8,128)} %get-tuple-element.9) | copy-start | bytes 737284

commit v3 on v2

--- a/solution.py
+++ b/solution.py
@@ -9,7 +9,7 @@
 from jax.sharding import PartitionSpec as P
 
 FR = 16
-REDUCERS = 24
+REDUCERS = 16
 epsilon = 1e-06
 masked = -1e30
 F32 = jnp.float32
@@ -76,7 +76,7 @@
     result, grad_result,
     video, prior, taps, basis, gain_s, gain_t, in_s, in_t, cot, perm, frame_bias, clip_bias, edge,
     part_a, part_b, part_c, land_a, land_b, land_c, full_a, full_b, full_c,
-    sent, got, back, home, gram, direct,
+    sent, got, sent_g, got_g, back, home, back_m, home_m, gram, direct,
     local_sem, send_sem, recv_sem,
 ):
     n_dp, n_ts, frames, places, columns, team, share, pad, rows, window = dims
@@ -119,15 +119,16 @@
         piece = ref.at[pl.ds(0, count)]
         pltpu.make_async_copy(piece, piece, sem).wait()
 
-    reducing = lax.rem(me, 4) != 3
-    inside = me < REDUCERS // 3 * 4
-    leads = jnp.logical_and(reducing, inside)
-    mine = (me // 4) * 3 + lax.rem(me, 4)
+    half, quarter = n_ts // 2, n_ts // 4
+    mine = dp * half + ts - quarter
+    leads = jnp.logical_and(
+        jnp.logical_and(ts >= quarter, ts < quarter + half), mine < REDUCERS
+    )
 
     def scatter(part, land, index):
         def step(i, carry):
             r = lax.rem(me + i, REDUCERS)
-            dev = r + r // 3
+            dev = r // half * n_ts + quarter + lax.rem(r, half)
 
             @pl.when(dev != me)
             def _():
@@ -164,7 +165,7 @@
             settle(full, REDUCERS, recv_sem.at[index + 1])
             settle(part, REDUCERS, send_sem.at[index])
 
-        return unstacked(full[...].reshape(-1, head))
+        return unstacked(full[...].astype(F32).reshape(-1, head)).astype(BF16)
 
     for copy in copies[:6]:
         copy.wait()
@@ -182,8 +183,8 @@
     span = basis[0 : 2 * head, pl.ds(start, window)].astype(F32)
     span_s = (span[:head] * gain_s[:, pl.ds(start, window)]).astype(BF16)
     span_t = (span * gain_t[:, pl.ds(start, window)]).astype(BF16)
-    part_a[...] = stacked(mm(span_s, spread_s)).astype(BF16).reshape(part_a.shape)
-    part_b[...] = stacked(mm(span_t, spread_t)).astype(BF16).reshape(part_b.shape)
+    part_a[...] = stacked(mm(span_s, spread_s)).reshape(part_a.shape).astype(BF16)
+    part_b[...] = stacked(mm(span_t, spread_t)).reshape(part_b.shape).astype(BF16)
     copies[6].wait()
 
     pl.semaphore_wait(barrier, n - 1)
@@ -251,6 +252,28 @@
     grad_mix_time = direct[:, head:].astype(BF16)
     grams = gram[...]
 
+    seat = lax.rem(ts, team)
+    base = me - seat
+    order = perm[...]
+
+    def swap(source_ref, target_ref, index):
+        def step(i, carry):
+            other = lax.rem(seat + i, team)
+            remote(source_ref.at[other], target_ref.at[seat], index, base + other).start()
+            return carry
+
+        lax.fori_loop(1, team, step, 0)
+        target_ref[pl.ds(seat, 1)] = source_ref[pl.ds(seat, 1)]
+
+    def dealt(values, ref):
+        ref[...] = mm(order, values).reshape(ref.shape).astype(BF16)
+
+    def received(ref, index):
+        settle(ref, team - 1, recv_sem.at[index])
+        return ref[...].astype(F32).reshape(team * pad, -1).astype(BF16)
+
+    dealt(grad_mix_time, sent_g)
+    swap(sent_g, got_g, 9)
     gather(part_b, land_b, full_b, 3)
 
     squares = jnp.sum(
@@ -268,35 +291,18 @@
     map_time = collect(part_b, land_b, full_b, 3)
     packed_two = (mm(joint, map_time) * factor_two).astype(BF16)
 
-    seat = lax.rem(ts, team)
-    base = me - seat
-    order = perm[...]
-
-    def swap(source_ref, target_ref, index):
-        def step(i, carry):
-            other = lax.rem(seat + i, team)
-            remote(source_ref.at[other], target_ref.at[seat], index, base + other).start()
-            return carry
-
-        lax.fori_loop(1, team, step, 0)
-        target_ref[pl.ds(seat, 1)] = source_ref[pl.ds(seat, 1)]
-
-    sent[...] = (
-        mm(order, jnp.concatenate([packed_two, grad_mix_time], axis=-1))
-        .astype(BF16)
-        .reshape(sent.shape)
-    )
+    dealt(packed_two, sent)
     swap(sent, got, 5)
-    settle(got, team - 1, recv_sem.at[5])
-    arrived = got[...].reshape(team * pad, 4 * head)
-    tq, tk, tv, tg = (arrived[:, i * head : (i + 1) * head] for i in range(4))
+    tg = received(got_g, 9)
+    arrived = received(got, 5)
+    tq, tk, tv = (arrived[:, i * head : (i + 1) * head] for i in range(3))
     mixture_two, attend_two = attend_forward(tq, tk, tv, clip_bias[...])
     grad_two = attend_backward(tq, tk, tv, attend_two, tg)
-    back[...] = jnp.concatenate([mixture_two, grad_two], axis=-1).reshape(back.shape)
+    back[...] = grad_two.astype(F32).reshape(back.shape).astype(BF16)
     swap(back, home, 6)
-    settle(home, team - 1, recv_sem.at[6])
-    returned = t_mm(order, home[...].reshape(team * pad, 4 * head)).astype(BF16)
-    mixture_two, grad_two = returned[:, :head], returned[:, head:]
+    back_m[...] = mixture_two.astype(F32).reshape(back_m.shape).astype(BF16)
+    swap(back_m, home_m, 10)
+    grad_two = t_mm(order, received(home, 6)).astype(BF16)
 
     inner = jnp.sum(grad_two.astype(F32) * packed_two.astype(F32), axis=-1, keepdims=True)
     grad_mix_one = (
@@ -306,19 +312,12 @@
     ).astype(BF16)
     grad_one = attend_backward(q, k, v, attend_one, grad_mix_one)
     scaled = (features.astype(F32) * factor_one).astype(BF16)
-    part_c[...] = stacked(t_mm(scaled, grad_one)).astype(BF16).reshape(part_c.shape)
+    part_c[...] = stacked(t_mm(scaled, grad_one)).reshape(part_c.shape).astype(BF16)
     scatter(part_c, land_c, 7)
 
-    triple = jnp.concatenate([joint, mixture_two], axis=-1)
-
-    def write(i, carry):
-        cols = pl.ds(pl.multiple_of(i * chunk, 128), chunk)
-        result[:, cols] = mm(triple, basis[:, cols]).astype(BF16)
-        return carry
-
-    lax.fori_loop(0, 2, write, 0)
+    mixture_two = t_mm(order, received(home_m, 10)).astype(BF16)
+    result[...] = jnp.concatenate([joint, mixture_two], axis=-1)
     gather(part_c, land_c, full_c, 7)
-    lax.fori_loop(2, 5, write, 0)
     total = collect(part_c, land_c, full_c, 7)
     grad_result[...] = t_mm(embed_rows, total)
 
@@ -328,6 +327,17 @@
 
     settle(sent, team - 1, send_sem.at[5])
     settle(back, team - 1, send_sem.at[6])
+    settle(sent_g, team - 1, send_sem.at[9])
+    settle(back_m, team - 1, send_sem.at[10])
+
+
+def final_kernel(factors, grad, embed, out_s, out_t, output, grad_result):
+    weight = jnp.concatenate([embed[...], out_s[...], out_t[...]], axis=0)
+    output[...] = mm(factors[...], weight).astype(BF16)
+
+    @pl.when(pl.program_id(0) == 0)
+    def _():
+        grad_result[...] = grad[...]
 
 
 def shards(
@@ -344,7 +354,7 @@
     n = n_dp * n_ts
     team = FR // frames
     share = places // team
-    pad = -(-frames * share // 16) * 16
+    pad = -(-frames * share // 8) * 8
     reach = max(i * rows % 128 + rows for i in range(n))
     window = -(-reach // 128) * 128
 
@@ -372,14 +382,14 @@
     edge[:, 3] = spot % columns < columns - 1
 
     dims = (n_dp, n_ts, frames, places, columns, team, share, pad, rows, window)
-    any_space = pl.BlockSpec(memory_space=pl.ANY)
+    any_space = pl.BlockSpec(memory_space=pltpu.HBM)
     vmem = pl.BlockSpec(memory_space=pltpu.VMEM)
     buffer = lambda *shape: pltpu.VMEM(shape, BF16)
     wide = lambda *shape: pltpu.VMEM(shape, F32)
-    output, grad = pl.pallas_call(
+    factors, grad = pl.pallas_call(
         functools.partial(whole_kernel, dims),
         out_shape=(
-            jax.ShapeDtypeStruct((tokens, width), BF16),
+            jax.ShapeDtypeStruct((tokens, 3 * head), BF16),
             jax.ShapeDtypeStruct((rows, triple), F32),
         ),
         in_specs=[any_space] * 14,
@@ -390,14 +400,16 @@
             buffer(rows, triple), buffer(rows, triple), buffer(tokens, width),
             buffer(team * pad, tokens), buffer(tokens, tokens), buffer(team * pad, team * pad),
             buffer(tokens, 128),
-            buffer(REDUCERS, 16, 128), buffer(REDUCERS, 32, 128), buffer(REDUCERS, 16, 128),
-            buffer(n, 16, 128), buffer(n, 32, 128), buffer(n, 16, 128),
-            buffer(REDUCERS, 16, 128), buffer(REDUCERS, 32, 128), buffer(REDUCERS, 16, 128),
-            buffer(team, pad, 4 * head), buffer(team, pad, 4 * head),
-            buffer(team, pad, 4 * head), buffer(team, pad, 4 * head),
+            buffer(REDUCERS, 24, 128), buffer(REDUCERS, 48, 128), buffer(REDUCERS, 24, 128),
+            buffer(n, 24, 128), buffer(n, 48, 128), buffer(n, 24, 128),
+            buffer(REDUCERS, 24, 128), buffer(REDUCERS, 48, 128), buffer(REDUCERS, 24, 128),
+            buffer(team, pad, triple), buffer(team, pad, triple),
+            buffer(team, pad, head), buffer(team, pad, head),
+            buffer(team, pad, triple), buffer(team, pad, triple),
+            buffer(team, pad, head), buffer(team, pad, head),
             wide(2 * head, 2 * head), wide(tokens, 2 * head),
-            pltpu.SemaphoreType.DMA((14,)), pltpu.SemaphoreType.DMA((9,)),
-            pltpu.SemaphoreType.DMA((9,)),
+            pltpu.SemaphoreType.DMA((14,)), pltpu.SemaphoreType.DMA((11,)),
+            pltpu.SemaphoreType.DMA((11,)),
         ],
         compiler_params=pltpu.CompilerParams(
             collective_id=0, has_side_effects=True, vmem_limit_bytes=56 * 1024 * 1024
@@ -418,6 +430,25 @@
         jnp.asarray(clip_bias, BF16),
         jnp.asarray(edge, BF16),
     )
+    chunk = width // 5
+    column = lambda i: (0, i)
+    fixed = lambda i: (0, 0)
+    output, grad = pl.pallas_call(
+        final_kernel,
+        grid=(5,),
+        out_shape=(
+            jax.ShapeDtypeStruct((tokens, width), BF16),
+            jax.ShapeDtypeStruct((rows, triple), F32),
+        ),
+        in_specs=[
+            pl.BlockSpec((tokens, 3 * head), fixed),
+            pl.BlockSpec((rows, triple), fixed),
+            pl.BlockSpec((head, chunk), column),
+            pl.BlockSpec((head, chunk), column),
+            pl.BlockSpec((head, chunk), column),
+        ],
+        out_specs=(pl.BlockSpec((tokens, chunk), column), pl.BlockSpec((rows, triple), fixed)),
+    )(factors, grad, embed_weight, output_spatial, output_temporal)
     return output.reshape(frames, height, columns, width), grad
 
 

time: 57.4 us -> 56.8 us (0.990)
  local copies, waits for them, and re-layouts: 4.58 us -> 0 us
  Pallas kernels: 52 us -> 55.9 us
    pallas_call x0 -> x1, Pallas kernels: none -> 6.54 us  [shards(): pl.pallas_call(final_kernel, grid=(5,), out_shape=(jax.ShapeDtypeStruct((...]
    unnamed x4 -> x0, local copies, waits for them, and re-layouts: 4.58 us -> none
    pallas_call x1, Pallas kernels: 52 us -> 49.4 us  [shards(): pl.pallas_call(functools.partial(whole_kernel, dims), out_shape=(jax.Shap...]
where the time goes in v3:
time: 56.8 us; the launch traced here: 56.5 us
  Pallas kernels  55.9 us (98%)
  between operations  0.64 us (1%)
    pallas_call x1, Pallas kernels, shards(): pl.pallas_call(functools.partial(whole_kernel, dims), out_shape=(jax.Shap...  49.4 us
    pallas_call x1, Pallas kernels, shards(): pl.pallas_call(final_kernel, grid=(5,), out_shape=(jax.ShapeDtypeStruct((...  6.54 us

profile of v3, /device:TPU:0, one launch (start us, length us, event | category | flops | bytes accessed | tf_op | source)
XLA Modules:
  0.0 56.5 jit_solution(15644615619145377083)
XLA Ops:
  0.6 49.4 %shard_map.149 = (bf16[320,384]{1,0:T(8,128)(2,1)}, f32[160,384]{1,0:T(8,128)}) custom-call(bf16[2,160,128]{2,1,0:T(8,128)(2,1)} %bitcast.6, bf16[3,3,3,128,128]{4,3,2,1,0:T(8,128)(2,1)} %conv_hbm.1, bf16[128,5120]{1,0:T(8,128)(2,1)} %embed.1, f32[1,5120]{1,0:T(1,128)} %bitcast.7, f32[1,5120]{1,0:T(1,128)} %bitcast.8, bf16[160,384]{1,0:T(8,128)(2,1)} %in_s_hbm.1, ...), custom_call_target="tpu_custom_call" | custom-call | tf_op jit(solution)/shard_map/pallas_call | solution.py:389
  50.0 6.5 %shard_map.150 = (bf16[320,5120]{1,0:T(8,128)(2,1)}, f32[160,384]{1,0:T(8,128)}) custom-call(bf16[320,384]{1,0:T(8,128)(2,1)} %get-tuple-element.6.factors, f32[160,384]{1,0:T(8,128)} %get-tuple-element.7.grad, bf16[128,5120]{1,0:T(8,128)(2,1)} %embed.1, bf16[128,5120]{1,0:T(8,128)(2,1)} %out_s.1, bf16[128,5120]{1,0:T(8,128)(2,1)} %out_t.1), custom_call_target="tpu_custom_call" | custom-call | tf_op jit(solution)/shard_map/pallas_call | solution.py:436

commit v4 on v3

--- a/solution.py
+++ b/solution.py
@@ -316,8 +316,16 @@
     scatter(part_c, land_c, 7)
 
     mixture_two = t_mm(order, received(home_m, 10)).astype(BF16)
-    result[...] = jnp.concatenate([joint, mixture_two], axis=-1)
+    triple = jnp.concatenate([joint, mixture_two], axis=-1)
+
+    def write(i, carry):
+        cols = pl.ds(pl.multiple_of(i * chunk, 128), chunk)
+        result[:, cols] = mm(triple, basis[:, cols]).astype(BF16)
+        return carry
+
+    lax.fori_loop(0, 2, write, 0)
     gather(part_c, land_c, full_c, 7)
+    lax.fori_loop(2, 5, write, 0)
     total = collect(part_c, land_c, full_c, 7)
     grad_result[...] = t_mm(embed_rows, total)
 
@@ -329,15 +337,6 @@
     settle(back, team - 1, send_sem.at[6])
     settle(sent_g, team - 1, send_sem.at[9])
     settle(back_m, team - 1, send_sem.at[10])
-
-
-def final_kernel(factors, grad, embed, out_s, out_t, output, grad_result):
-    weight = jnp.concatenate([embed[...], out_s[...], out_t[...]], axis=0)
-    output[...] = mm(factors[...], weight).astype(BF16)
-
-    @pl.when(pl.program_id(0) == 0)
-    def _():
-        grad_result[...] = grad[...]
 
 
 def shards(
@@ -386,10 +385,10 @@
     vmem = pl.BlockSpec(memory_space=pltpu.VMEM)
     buffer = lambda *shape: pltpu.VMEM(shape, BF16)
     wide = lambda *shape: pltpu.VMEM(shape, F32)
-    factors, grad = pl.pallas_call(
+    output, grad = pl.pallas_call(
         functools.partial(whole_kernel, dims),
         out_shape=(
-            jax.ShapeDtypeStruct((tokens, 3 * head), BF16),
+            jax.ShapeDtypeStruct((tokens, width), BF16),
             jax.ShapeDtypeStruct((rows, triple), F32),
         ),
         in_specs=[any_space] * 14,
@@ -412,9 +411,9 @@
             pltpu.SemaphoreType.DMA((11,)),
         ],
         compiler_params=pltpu.CompilerParams(
-            collective_id=0, has_side_effects=True, vmem_limit_bytes=56 * 1024 * 1024
+            collective_id=0, has_side_effects=True, vmem_limit_bytes=36 * 1024 * 1024
         ),
-    )(
+    )(*(pltpu.with_memory_space_constraint(x, pltpu.HBM) for x in (
         clip_video.reshape(frames, places, channels),
         conv_weight,
         embed_weight,
@@ -429,26 +428,7 @@
         jnp.asarray(frame_bias, BF16),
         jnp.asarray(clip_bias, BF16),
         jnp.asarray(edge, BF16),
-    )
-    chunk = width // 5
-    column = lambda i: (0, i)
-    fixed = lambda i: (0, 0)
-    output, grad = pl.pallas_call(
-        final_kernel,
-        grid=(5,),
-        out_shape=(
-            jax.ShapeDtypeStruct((tokens, width), BF16),
-            jax.ShapeDtypeStruct((rows, triple), F32),
-        ),
-        in_specs=[
-            pl.BlockSpec((tokens, 3 * head), fixed),
-            pl.BlockSpec((rows, triple), fixed),
-            pl.BlockSpec((head, chunk), column),
-            pl.BlockSpec((head, chunk), column),
-            pl.BlockSpec((head, chunk), column),
-        ],
-        out_specs=(pl.BlockSpec((tokens, chunk), column), pl.BlockSpec((rows, triple), fixed)),
-    )(factors, grad, embed_weight, output_spatial, output_temporal)
+    )))
     return output.reshape(frames, height, columns, width), grad
 
 

time: 56.8 us -> 51.8 us (0.912)
  Pallas kernels: 55.9 us -> 48.6 us
  local copies, waits for them, and re-layouts: 0 us -> 2.4 us
    pallas_call x1 -> x0, Pallas kernels: 6.54 us -> none  [shards(): pl.pallas_call(final_kernel, grid=(5,), out_shape=(jax.ShapeDtypeStruct((...]
    unnamed x0 -> x2, local copies, waits for them, and re-layouts: none -> 2.4 us
    pallas_call x1, Pallas kernels: 49.4 us -> 48.6 us  [shards(): pl.pallas_call(functools.partial(whole_kernel, dims), out_shape=(jax.Shap...]
where the time goes in v4:
time: 51.8 us; the launch traced here: 51.6 us
  Pallas kernels  48.6 us (94%)
  local copies, waits for them, and re-layouts  2.4 us (5%)
  between operations  0.64 us (1%)
    pallas_call x1, Pallas kernels, shards(): pl.pallas_call(functools.partial(whole_kernel, dims), out_shape=(jax.Shap...  48.6 us
    unnamed x2, local copies, waits for them, and re-layouts  2.4 us

profile of v4, /device:TPU:0, one launch (start us, length us, event | category | flops | bytes accessed | tf_op | source)
XLA Modules:
  0.0 51.6 jit_solution(13443320515524589683)
XLA Ops:
  0.6 48.6 %shard_map.149 = (bf16[320,5120]{1,0:T(8,128)(2,1)S(1)}, f32[160,384]{1,0:T(8,128)S(1)}) custom-call(bf16[2,160,128]{2,1,0:T(8,128)(2,1)} %bitcast.7, bf16[3,3,3,128,128]{4,3,2,1,0:T(8,128)(2,1)} %conv_hbm.1, bf16[128,5120]{1,0:T(8,128)(2,1)} %embed_hbm.1, f32[1,5120]{1,0:T(1,128)} %bitcast.8, f32[1,5120]{1,0:T(1,128)} %bitcast.9, ...), custom_call_target="tpu_custom_call" | custom-call | tf_op jit(solution)/shard_map/pallas_call | solution.py:388
  49.2 1.7 %copy.18 = bf16[2,4,40,5120]{3,2,1,0:T(8,128)(2,1)} copy(bf16[2,4,40,5120]{3,2,1,0:T(8,128)(2,1)S(1)} %bitcast.5) | data formatting | bytes 6553600
  50.9 0.7 %copy.19 = f32[160,384]{1,0:T(8,128)} copy(f32[160,384]{1,0:T(8,128)S(1)} %get-tuple-element.9) | data formatting | bytes 491520

commit v5 on v4

--- a/solution.py
+++ b/solution.py
@@ -75,7 +75,7 @@
     out_t_hbm, cot_hbm, perm_hbm, frame_bias_hbm, clip_bias_hbm, edge_hbm,
     result, grad_result,
     video, prior, taps, basis, gain_s, gain_t, in_s, in_t, cot, perm, frame_bias, clip_bias, edge,
-    part_a, part_b, part_c, land_a, land_b, land_c, full_a, full_b, full_c,
+    twin_a, twin_b, pre_a, pre_b, part_a, part_b, part_c, land_a, land_b, land_c, full_a, full_b, full_c,
     sent, got, sent_g, got_g, back, home, back_m, home_m, gram, direct,
     local_sem, send_sem, recv_sem,
 ):
@@ -120,15 +120,23 @@
         pltpu.make_async_copy(piece, piece, sem).wait()
 
     half, quarter = n_ts // 2, n_ts // 4
-    mine = dp * half + ts - quarter
+    core = lax.rem(ts, 2)
+    partner = me + 1 - 2 * core
+    pairs = REDUCERS // 2
+    seated = dp * (half // 2) + (ts - quarter) // 2
+    mine = core * pairs + seated
+
+    def leader(side, i):
+        return i // (half // 2) * n_ts + quarter + 2 * lax.rem(i, half // 2) + side
+
     leads = jnp.logical_and(
-        jnp.logical_and(ts >= quarter, ts < quarter + half), mine < REDUCERS
+        jnp.logical_and(ts >= quarter, ts < quarter + half), seated < pairs
     )
 
     def scatter(part, land, index):
         def step(i, carry):
             r = lax.rem(me + i, REDUCERS)
-            dev = r // half * n_ts + quarter + lax.rem(r, half)
+            dev = leader(r // pairs, lax.rem(r, pairs))
 
             @pl.when(dev != me)
             def _():
@@ -165,6 +173,61 @@
             settle(full, REDUCERS, recv_sem.at[index + 1])
             settle(part, REDUCERS, send_sem.at[index])
 
+        return unstacked(full[...].astype(F32).reshape(-1, head)).astype(BF16)
+
+    def pair_start(part, twin, index):
+        other = pl.ds((1 - core) * pairs, pairs)
+        remote(part.at[other], twin, index, partner).start()
+
+    def pair_scatter(part, twin, pre, land, index, pair_index):
+        settle(twin, pairs, recv_sem.at[pair_index])
+        own = part[pl.ds(core * pairs, pairs)].astype(F32)
+        pre[...] = (own + twin[...].astype(F32)).astype(BF16)
+
+        def step(i, carry):
+            r = lax.rem(me // 2 + i, pairs)
+            dev = leader(core, r)
+
+            @pl.when(dev != me)
+            def _():
+                remote(pre.at[r], land.at[me // 2], index, dev).start()
+
+            return carry
+
+        lax.fori_loop(0, pairs, step, 0)
+
+    def pair_gather(pre, land, full, index):
+        @pl.when(leads)
+        def _():
+            land[pl.ds(me // 2, 1)] = pre[pl.ds(seated, 1)]
+            settle(land, n // 2 - 1, recv_sem.at[index])
+            total = jnp.sum(land[...].astype(F32), axis=0, keepdims=True)
+            full[pl.ds(mine, 1)] = total.astype(BF16)
+
+            def step(i, carry):
+                dev = 2 * lax.rem(me // 2 + i, n // 2) + core
+                remote(full.at[mine], full.at[mine], index + 1, dev).start()
+                return carry
+
+            lax.fori_loop(1, n // 2, step, 0)
+
+    def pair_collect(pre, twin, land, full, index, pair_index):
+        @pl.when(leads)
+        def _():
+            settle(full, pairs - 1, recv_sem.at[index + 1])
+            settle(pre, pairs - 1, send_sem.at[index])
+            settle(land, n // 2 - 1, send_sem.at[index + 1])
+
+        @pl.when(jnp.logical_not(leads))
+        def _():
+            settle(full, pairs, recv_sem.at[index + 1])
+            settle(pre, pairs, send_sem.at[index])
+
+        own = pl.ds(core * pairs, pairs)
+        remote(full.at[own], full.at[own], pair_index + 2, partner).start()
+        settle(full, pairs, recv_sem.at[pair_index + 2])
+        settle(twin, pairs, send_sem.at[pair_index])
+        settle(full, pairs, send_sem.at[pair_index + 2])
         return unstacked(full[...].astype(F32).reshape(-1, head)).astype(BF16)
 
     for copy in copies[:6]:
@@ -195,8 +258,10 @@
     def _():
         halo.start()
 
-    scatter(part_a, land_a, 1)
-    scatter(part_b, land_b, 3)
+    pair_start(part_a, twin_a, 11)
+    pair_start(part_b, twin_b, 12)
+    pair_scatter(part_a, twin_a, pre_a, land_a, 1, 11)
+    pair_scatter(part_b, twin_b, pre_b, land_b, 3, 12)
     embed_rows = mm(span_s, chosen).astype(BF16)
 
     @pl.when(ts == 0)
@@ -233,7 +298,7 @@
     )
     features = jax.nn.gelu(summed, approximate=True).astype(BF16)
 
-    gather(part_a, land_a, full_a, 1)
+    pair_gather(pre_a, land_a, full_a, 1)
 
     for copy in copies[11:]:
         copy.wait()
@@ -274,13 +339,13 @@
 
     dealt(grad_mix_time, sent_g)
     swap(sent_g, got_g, 9)
-    gather(part_b, land_b, full_b, 3)
+    pair_gather(pre_b, land_b, full_b, 3)
 
     squares = jnp.sum(
         wide_mm(features, grams[:head, :head]) * features.astype(F32), axis=-1, keepdims=True
     )
     factor_one = lax.rsqrt(jnp.maximum(squares, 0.0) / width + epsilon)
-    map_space = collect(part_a, land_a, full_a, 1)
+    map_space = pair_collect(pre_a, twin_a, land_a, full_a, 1, 11)
     packed_one = (mm(features, map_space) * factor_one).astype(BF16)
     q, k, v = packed_one[:, :head], packed_one[:, head : 2 * head], packed_one[:, 2 * head :]
     mixture_one, attend_one = attend_forward(q, k, v, frame_bias[...])
@@ -288,7 +353,7 @@
     spread = wide_mm(joint, grams)
     squares = jnp.sum(spread * joint.astype(F32), axis=-1, keepdims=True)
     factor_two = lax.rsqrt(jnp.maximum(squares, 0.0) / width + epsilon)
-    map_time = collect(part_b, land_b, full_b, 3)
+    map_time = pair_collect(pre_b, twin_b, land_b, full_b, 3, 12)
     packed_two = (mm(joint, map_time) * factor_two).astype(BF16)
 
     dealt(packed_two, sent)
@@ -399,16 +464,18 @@
             buffer(rows, triple), buffer(rows, triple), buffer(tokens, width),
             buffer(team * pad, tokens), buffer(tokens, tokens), buffer(team * pad, team * pad),
             buffer(tokens, 128),
+            buffer(REDUCERS // 2, 24, 128), buffer(REDUCERS // 2, 48, 128),
+            buffer(REDUCERS // 2, 24, 128), buffer(REDUCERS // 2, 48, 128),
             buffer(REDUCERS, 24, 128), buffer(REDUCERS, 48, 128), buffer(REDUCERS, 24, 128),
-            buffer(n, 24, 128), buffer(n, 48, 128), buffer(n, 24, 128),
+            buffer(n // 2, 24, 128), buffer(n // 2, 48, 128), buffer(n, 24, 128),
             buffer(REDUCERS, 24, 128), buffer(REDUCERS, 48, 128), buffer(REDUCERS, 24, 128),
             buffer(team, pad, triple), buffer(team, pad, triple),
             buffer(team, pad, head), buffer(team, pad, head),
             buffer(team, pad, triple), buffer(team, pad, triple),
             buffer(team, pad, head), buffer(team, pad, head),
             wide(2 * head, 2 * head), wide(tokens, 2 * head),
-            pltpu.SemaphoreType.DMA((14,)), pltpu.SemaphoreType.DMA((11,)),
-            pltpu.SemaphoreType.DMA((11,)),
+            pltpu.SemaphoreType.DMA((14,)), pltpu.SemaphoreType.DMA((15,)),
+            pltpu.SemaphoreType.DMA((15,)),
         ],
         compiler_params=pltpu.CompilerParams(
             collective_id=0, has_side_effects=True, vmem_limit_bytes=36 * 1024 * 1024

time: 51.8 us -> 47.1 us (0.909)
  Pallas kernels: 48.6 us -> 43.9 us
    pallas_call x1, Pallas kernels: 48.6 us -> 43.9 us  [shards(): pl.pallas_call(functools.partial(whole_kernel, dims), out_shape=(jax.Shap...]
where the time goes in v5:
time: 47.1 us; the launch traced here: 46.9 us
  Pallas kernels  43.9 us (93%)
  local copies, waits for them, and re-layouts  2.4 us (5%)
  between operations  0.64 us (1%)
    pallas_call x1, Pallas kernels, shards(): pl.pallas_call(functools.partial(whole_kernel, dims), out_shape=(jax.Shap...  43.9 us
    unnamed x2, local copies, waits for them, and re-layouts  2.4 us

profile of v5, /device:TPU:0, one launch (start us, length us, event | category | flops | bytes accessed | tf_op | source)
XLA Modules:
  0.0 46.9 jit_solution(15364165928580215267)
XLA Ops:
  0.6 43.9 %shard_map.149 = (bf16[320,5120]{1,0:T(8,128)(2,1)S(1)}, f32[160,384]{1,0:T(8,128)S(1)}) custom-call(bf16[2,160,128]{2,1,0:T(8,128)(2,1)} %bitcast.7, bf16[3,3,3,128,128]{4,3,2,1,0:T(8,128)(2,1)} %conv_hbm.1, bf16[128,5120]{1,0:T(8,128)(2,1)} %embed_hbm.1, f32[1,5120]{1,0:T(1,128)} %bitcast.8, f32[1,5120]{1,0:T(1,128)} %bitcast.9, ...), custom_call_target="tpu_custom_call" | custom-call | tf_op jit(solution)/shard_map/pallas_call | solution.py:453
  44.5 1.7 %copy.18 = bf16[2,4,40,5120]{3,2,1,0:T(8,128)(2,1)} copy(bf16[2,4,40,5120]{3,2,1,0:T(8,128)(2,1)S(1)} %bitcast.5) | data formatting | bytes 6553600
  46.2 0.7 %copy.19 = f32[160,384]{1,0:T(8,128)} copy(f32[160,384]{1,0:T(8,128)S(1)} %get-tuple-element.9) | data formatting | bytes 491520

commit v6 on v5

--- a/solution.py
+++ b/solution.py
@@ -75,7 +75,7 @@
     out_t_hbm, cot_hbm, perm_hbm, frame_bias_hbm, clip_bias_hbm, edge_hbm,
     result, grad_result,
     video, prior, taps, basis, gain_s, gain_t, in_s, in_t, cot, perm, frame_bias, clip_bias, edge,
-    twin_a, twin_b, pre_a, pre_b, part_a, part_b, part_c, land_a, land_b, land_c, full_a, full_b, full_c,
+    twin_c, pre_c, twin_a, twin_b, pre_a, pre_b, part_a, part_b, part_c, land_a, land_b, land_c, full_a, full_b, full_c,
     sent, got, sent_g, got_g, back, home, back_m, home_m, gram, direct,
     local_sem, send_sem, recv_sem,
 ):
@@ -378,7 +378,8 @@
     grad_one = attend_backward(q, k, v, attend_one, grad_mix_one)
     scaled = (features.astype(F32) * factor_one).astype(BF16)
     part_c[...] = stacked(t_mm(scaled, grad_one)).reshape(part_c.shape).astype(BF16)
-    scatter(part_c, land_c, 7)
+    pair_start(part_c, twin_c, 15)
+    pair_scatter(part_c, twin_c, pre_c, land_c, 7, 15)
 
     mixture_two = t_mm(order, received(home_m, 10)).astype(BF16)
     triple = jnp.concatenate([joint, mixture_two], axis=-1)
@@ -389,9 +390,9 @@
         return carry
 
     lax.fori_loop(0, 2, write, 0)
-    gather(part_c, land_c, full_c, 7)
+    pair_gather(pre_c, land_c, full_c, 7)
     lax.fori_loop(2, 5, write, 0)
-    total = collect(part_c, land_c, full_c, 7)
+    total = pair_collect(pre_c, twin_c, land_c, full_c, 7, 15)
     grad_result[...] = t_mm(embed_rows, total)
 
     @pl.when(ts < n_ts - 1)
@@ -464,18 +465,19 @@
             buffer(rows, triple), buffer(rows, triple), buffer(tokens, width),
             buffer(team * pad, tokens), buffer(tokens, tokens), buffer(team * pad, team * pad),
             buffer(tokens, 128),
+            buffer(REDUCERS // 2, 24, 128), buffer(REDUCERS // 2, 24, 128),
             buffer(REDUCERS // 2, 24, 128), buffer(REDUCERS // 2, 48, 128),
             buffer(REDUCERS // 2, 24, 128), buffer(REDUCERS // 2, 48, 128),
             buffer(REDUCERS, 24, 128), buffer(REDUCERS, 48, 128), buffer(REDUCERS, 24, 128),
-            buffer(n // 2, 24, 128), buffer(n // 2, 48, 128), buffer(n, 24, 128),
+            buffer(n // 2, 24, 128), buffer(n // 2, 48, 128), buffer(n // 2, 24, 128),
             buffer(REDUCERS, 24, 128), buffer(REDUCERS, 48, 128), buffer(REDUCERS, 24, 128),
             buffer(team, pad, triple), buffer(team, pad, triple),
             buffer(team, pad, head), buffer(team, pad, head),
             buffer(team, pad, triple), buffer(team, pad, triple),
             buffer(team, pad, head), buffer(team, pad, head),
             wide(2 * head, 2 * head), wide(tokens, 2 * head),
-            pltpu.SemaphoreType.DMA((14,)), pltpu.SemaphoreType.DMA((15,)),
-            pltpu.SemaphoreType.DMA((15,)),
+            pltpu.SemaphoreType.DMA((14,)), pltpu.SemaphoreType.DMA((18,)),
+            pltpu.SemaphoreType.DMA((18,)),
         ],
         compiler_params=pltpu.CompilerParams(
             collective_id=0, has_side_effects=True, vmem_limit_bytes=36 * 1024 * 1024

time: 47.1 us -> 47.9 us (1.017)
  Pallas kernels: 43.9 us -> 44.8 us
    pallas_call x1, Pallas kernels: 43.9 us -> 44.8 us  [shards(): pl.pallas_call(functools.partial(whole_kernel, dims), out_shape=(jax.Shap...]
where the time goes in v6:
time: 47.9 us; the launch traced here: 47.8 us
  Pallas kernels  44.8 us (94%)
  local copies, waits for them, and re-layouts  2.4 us (5%)
  between operations  0.64 us (1%)
    pallas_call x1, Pallas kernels, shards(): pl.pallas_call(functools.partial(whole_kernel, dims), out_shape=(jax.Shap...  44.8 us
    unnamed x2, local copies, waits for them, and re-layouts  2.4 us

profile of v6, /device:TPU:0, one launch (start us, length us, event | category | flops | bytes accessed | tf_op | source)
XLA Modules:
  0.0 47.8 jit_solution(9906259504883573835)
XLA Ops:
  0.6 44.8 %shard_map.149 = (bf16[320,5120]{1,0:T(8,128)(2,1)S(1)}, f32[160,384]{1,0:T(8,128)S(1)}) custom-call(bf16[2,160,128]{2,1,0:T(8,128)(2,1)} %bitcast.7, bf16[3,3,3,128,128]{4,3,2,1,0:T(8,128)(2,1)} %conv_hbm.1, bf16[128,5120]{1,0:T(8,128)(2,1)} %embed_hbm.1, f32[1,5120]{1,0:T(1,128)} %bitcast.8, f32[1,5120]{1,0:T(1,128)} %bitcast.9, ...), custom_call_target="tpu_custom_call" | custom-call | tf_op jit(solution)/shard_map/pallas_call | solution.py:454
  45.4 1.7 %copy.18 = bf16[2,4,40,5120]{3,2,1,0:T(8,128)(2,1)} copy(bf16[2,4,40,5120]{3,2,1,0:T(8,128)(2,1)S(1)} %bitcast.5) | data formatting | bytes 6553600
  47.1 0.7 %copy.19 = f32[160,384]{1,0:T(8,128)} copy(f32[160,384]{1,0:T(8,128)S(1)} %get-tuple-element.9) | data formatting | bytes 491520
